TPU v7x, 32 devices: a whole 2x2x4 slice. The times are simulated.
32 devices in a mesh: dp: 16 (over z, y, x), tensor: 2 (over core).
Axes of the slice: x: 2, y: 2, z: 4, core: 2. Of those that a mesh axis runs over, the one named last changes fastest.
Arguments:
- tokens: bfloat16 [16384, 768], P(('dp', 'tensor')), may hold values from -6 to 6
- cotangent: bfloat16 [16384, 768], P(('dp', 'tensor')), may hold values from -6 to 6
- gain_attn: float32 [768], replicated, may hold values from 0.5 to 1.5
- gain_ffn: float32 [768], replicated, may hold values from 0.5 to 1.5
- route_query: float32 [768], replicated, may hold values from -0.21875 to 0.21875
- route_key: float32 [768], replicated, may hold values from -0.21875 to 0.21875
- route_ffn: float32 [768], replicated, may hold values from -0.21875 to 0.21875
- light_query: bfloat16 [768, 512], P(None, 'tensor'), may hold values from -0.21875 to 0.21875
- light_key: bfloat16 [768, 512], P(None, 'tensor'), may hold values from -0.21875 to 0.21875
- light_value: bfloat16 [768, 512], P(None, 'tensor'), may hold values from -0.21875 to 0.21875
- light_out: bfloat16 [512, 768], P('tensor'), may hold values from -1 to 1
- heavy_query: bfloat16 [768, 768], P(None, 'tensor'), may hold values from -0.21875 to 0.21875
- heavy_key: bfloat16 [768, 768], P(None, 'tensor'), may hold values from -0.21875 to 0.21875
- heavy_value: bfloat16 [768, 768], P(None, 'tensor'), may hold values from -0.21875 to 0.21875
- heavy_out: bfloat16 [768, 768], P('tensor'), may hold values from -1.25 to 1.25
- light_gate: bfloat16 [768, 1024], P(None, 'tensor'), may hold values from -0.21875 to 0.21875
- light_up: bfloat16 [768, 1024], P(None, 'tensor'), may hold values from -0.21875 to 0.21875
- light_down: bfloat16 [1024, 768], P('tensor'), may hold values from -0.25 to 0.25
- heavy_gate: bfloat16 [768, 4096], P(None, 'tensor'), may hold values from -0.21875 to 0.21875
- heavy_up: bfloat16 [768, 4096], P(None, 'tensor'), may hold values from -0.21875 to 0.21875
- heavy_down: bfloat16 [4096, 768], P('tensor'), may hold values from -0.1875 to 0.1875
- query_index: int32 [16, 128], P('dp'), may hold values from 0 to 1023, as said below
- key_index: int32 [16, 128], P('dp'), may hold values from 0 to 1023, as said below
- ffn_index: int32 [16, 128], P('dp'), may hold values from 0 to 1023, as said below
Outputs:
- block_out: bfloat16 [16384, 768], P(('dp', 'tensor'))
- input_grad: bfloat16 [16384, 768], P(('dp', 'tensor'))
- gain_attn_grad: float32 [768], replicated
- gain_ffn_grad: float32 [768], replicated
- route_query_grad: float32 [768], replicated
- route_key_grad: float32 [768], replicated
- route_ffn_grad: float32 [768], replicated
- light_query_grad: float32 [768, 512], P('dp', 'tensor')
- light_key_grad: float32 [768, 512], P('dp', 'tensor')
- light_value_grad: float32 [768, 512], P('dp', 'tensor')
- light_out_grad: float32 [512, 768], P('tensor', 'dp')
- heavy_query_grad: float32 [768, 768], P('dp', 'tensor')
- heavy_key_grad: float32 [768, 768], P('dp', 'tensor')
- heavy_value_grad: float32 [768, 768], P('dp', 'tensor')
- heavy_out_grad: float32 [768, 768], P('tensor', 'dp')
- light_gate_grad: float32 [768, 1024], P('dp', 'tensor')
- light_up_grad: float32 [768, 1024], P('dp', 'tensor')
- light_down_grad: float32 [1024, 768], P('tensor', 'dp')
- heavy_gate_grad: float32 [768, 4096], P('dp', 'tensor')
- heavy_up_grad: float32 [768, 4096], P('dp', 'tensor')
- heavy_down_grad: float32 [4096, 768], P('tensor', 'dp')
Inputs may be any that keep to these rules, and one draw needn't show every extreme that they name: `query_index`: row s lists 128 different positions of sequence s. `key_index`: row s lists 128 different positions of sequence s. `ffn_index`: row s lists 128 different positions of sequence s.
All inputs are finite; a program needn't handle non-finite values.
Results may differ from a plain program's by a relative error of at most 0.018.
Values may be sent and summed in bfloat16 or wider, within the bound.
No kernel may reach another device: no remote copies, remote signals or barrier semaphores. Data moves between devices by JAX's collectives and lax.ppermute only.
A program may use at most 192 MiB of HBM per device.

v0:
```python
import jax
import jax.numpy as jnp
from jax import lax
from jax.experimental import pallas as pl
from jax.experimental.pallas import tpu as pltpu
from jax.sharding import PartitionSpec as P

HEAD_DIM = 64
WINDOW = 128
EPS = 1e-06
VMEM_LIMIT = 60 * 1024 * 1024
f32 = jnp.float32
bf16 = jnp.bfloat16


def pair_swap(values):
    return lax.ppermute(values, "tensor", [(0, 1), (1, 0)])


def halving_sum(values, order):
    parts = lax.axis_size("dp")
    place = lax.axis_index("dp")
    bits = list(range(len(order) - 1, -1, -1))
    held = values.reshape((2,) * len(bits) + (values.shape[0] // parts, values.shape[1]))
    held = held.astype(jnp.bfloat16)
    for step, bit in enumerate(order):
        axis = bits.index(bit)
        bits.remove(bit)
        mine = (place >> bit) & 1
        keep = lax.dynamic_index_in_dim(held, mine, axis, keepdims=False)
        send = lax.dynamic_index_in_dim(held, 1 - mine, axis, keepdims=False)
        got = lax.ppermute(send, "dp", [(i, i ^ (1 << bit)) for i in range(parts)])
        held = keep.astype(jnp.float32) + got.astype(jnp.float32)
        if step < len(order) - 1:
            held = held.astype(jnp.bfloat16)
    return held


def butterfly_sum(values):
    parts = lax.axis_size("dp")
    values = values + pair_swap(values)
    for bit in range(parts.bit_length() - 1):
        values = values + lax.ppermute(values, "dp", [(i, i ^ (1 << bit)) for i in range(parts)])
    return values


def mm(left, right, left_dim=1, right_dim=0):
    return lax.dot_general(
        left, right, (((left_dim,), (right_dim,)), ((), ())), preferred_element_type=f32
    )


def split_low(values):
    high = values.astype(bf16)
    return high, (values - high.astype(f32)).astype(bf16)


def sigmoid(values):
    return 1.0 / (1.0 + jnp.exp(-values))


def row_factor(values):
    return lax.rsqrt(jnp.mean(values * values, axis=-1, keepdims=True) + EPS)


def picks(index_ref, length):
    rows = lax.broadcasted_iota(jnp.int32, (length, index_ref.shape[1]), 0)
    return jnp.where(rows == index_ref[...], 1.0, 0.0).astype(bf16)


def head_masks(width):
    lanes = lax.shift_right_logical(lax.broadcasted_iota(jnp.int32, (1, width), 1), 6)
    return [jnp.where(lanes == head, 1.0, 0.0).astype(f32) for head in range(width // HEAD_DIM)]


def stack_heads(values, masks):
    return jnp.concatenate([values * mask.astype(values.dtype) for mask in masks], axis=0)


def unstack_heads(values, masks):
    rows = values.shape[0] // len(masks)
    total = values[:rows] * masks[0]
    for head in range(1, len(masks)):
        total = total + values[head * rows : (head + 1) * rows] * masks[head]
    return total


def softmax_rows(scores, axis):
    exponent = jnp.exp(scores - jnp.max(scores, axis=axis, keepdims=True))
    return exponent * (1.0 / jnp.sum(exponent, axis=axis, keepdims=True))


def window_start(block, length):
    start = jnp.clip(block * WINDOW - WINDOW, 0, length - 3 * WINDOW)
    return pl.multiple_of(start, WINDOW)


def attn_forward_kernel(
    own_ref,
    other_ref,
    gain_ref,
    route_query_ref,
    route_key_ref,
    query_index_ref,
    key_index_ref,
    wq_ref,
    wk_ref,
    wv_ref,
    wo_ref,
    hq_ref,
    hk_ref,
    hv_ref,
    ho_ref,
    partial_ref,
    input_ref,
    q_ref,
    k_ref,
    v_ref,
    result_ref,
    query_rows_ref,
    key_raw_ref,
    key_rows_ref,
    qh_ref,
    kh_ref,
    vh_ref,
    raw_ref,
    heavy_result_ref,
    pick_ref,
):
    side = lax.axis_index("tensor")
    half = own_ref.shape[0]
    length = 2 * half
    tile = 256
    for ref, place in ((own_ref, side), (other_ref, 1 - side)):
        for start in range(0, half, tile):
            values = ref[start : start + tile, :].astype(f32)
            normed = values * row_factor(values) * gain_ref[...]
            rows = pl.ds(pl.multiple_of(place * half + start, tile), tile)
            input_ref[rows, :] = normed.astype(bf16)
    routed = query_index_ref.shape[1]
    pick_ref[:, :routed] = picks(query_index_ref, length)
    pick_ref[:, routed:] = picks(key_index_ref, length)
    picked = mm(pick_ref[...], input_ref[...], 0, 0)
    query_rows = picked[:routed]
    key_raw = picked[routed:]
    query_score = sigmoid(jnp.sum(query_rows * route_query_ref[...], axis=-1, keepdims=True))
    key_score = sigmoid(jnp.sum(key_raw * route_key_ref[...], axis=-1, keepdims=True))
    query_rows_ref[...] = query_rows.astype(bf16)
    key_raw_ref[...] = key_raw.astype(bf16)
    key_rows_ref[...] = (key_score * key_raw).astype(bf16)
    qh_ref[...] = mm(query_rows_ref[...], hq_ref[...]).astype(bf16)
    kh_ref[...] = mm(key_rows_ref[...], hk_ref[...]).astype(bf16)
    vh_ref[...] = mm(key_rows_ref[...], hv_ref[...]).astype(bf16)
    pair = 2 * HEAD_DIM
    pair_masks = head_masks(pair)
    for start in range(0, qh_ref.shape[1], pair):
        cols = slice(start, start + pair)
        stacked = stack_heads(qh_ref[:, cols] * (HEAD_DIM**-0.5), pair_masks)
        probs = softmax_rows(mm(stacked, kh_ref[:, cols], 1, 1), -1)
        raw_ref[:, cols] = unstack_heads(mm(probs.astype(bf16), vh_ref[:, cols]), pair_masks)
    heavy_result_ref[...] = (query_score * raw_ref[...]).astype(bf16)
    high, low = split_low(mm(heavy_result_ref[...], ho_ref[...]))

    for start in range(0, length, tile):
        rows = slice(start, start + tile)
        q_ref[rows, :] = mm(input_ref[rows, :], wq_ref[...]).astype(bf16)
        k_ref[rows, :] = mm(input_ref[rows, :], wk_ref[...]).astype(bf16)
        v_ref[rows, :] = mm(input_ref[rows, :], wv_ref[...]).astype(bf16)

    masks = head_masks(q_ref.shape[1])
    heads = len(masks)
    gap = lax.broadcasted_iota(jnp.int32, (WINDOW, 3 * WINDOW), 0) - lax.broadcasted_iota(
        jnp.int32, (WINDOW, 3 * WINDOW), 1
    )

    def one_block(block, carry):
        rows = pl.ds(pl.multiple_of(block * WINDOW, WINDOW), WINDOW)
        start = window_start(block, length)
        keys = pl.ds(start, 3 * WINDOW)
        stacked = stack_heads(q_ref[rows, :] * (HEAD_DIM**-0.5), masks)
        scores = mm(stacked, k_ref[keys, :], 1, 1)
        near = jnp.abs(gap + (block * WINDOW - start)) < WINDOW
        bias = jnp.where(near, 0.0, -1e30)
        probs = softmax_rows(scores + jnp.concatenate([bias] * heads, axis=0), -1)
        out = unstack_heads(mm(probs.astype(bf16), v_ref[keys, :]), masks)
        result_ref[rows, :] = out.astype(bf16)
        return carry

    lax.fori_loop(0, length // WINDOW, one_block, 0)
    for start in range(0, length, tile):
        rows = slice(start, start + tile)
        pick = pick_ref[rows, :routed]
        partial_ref[rows, :] = (
            mm(result_ref[rows, :], wo_ref[...]) + (mm(pick, high) + mm(pick, low))
        ).astype(bf16)


def gelu_parts(values):
    density = jnp.exp(-0.5 * values * values) * 0.3989422804014327
    below = 0.5 * (1.0 + lax.erf(values * 0.7071067811865476))
    return values * below, below + values * density


def ffn_kernel(
    own_ref,
    other_ref,
    mine_ref,
    got_ref,
    cot_own_ref,
    cot_other_ref,
    gain_ref,
    route_ref,
    index_ref,
    wg_ref,
    wu_ref,
    wd_ref,
    hg_ref,
    hu_ref,
    hd_ref,
    middle_ref,
    block_own_ref,
    block_send_ref,
    back_ref,
    light_grad_ref,
    rows_ref,
    cot_rows_ref,
    act_heavy_ref,
    mix_heavy_ref,
    route_grad_ref,
    input_ref,
    cot_ref,
    act_ref,
    mix_ref,
    pick_ref,
):
    side = lax.axis_index("tensor")
    half = own_ref.shape[0]
    length = 2 * half
    tile = 256
    for ref, cot, place in ((own_ref, cot_own_ref, side), (other_ref, cot_other_ref, 1 - side)):
        for start in range(0, half, tile):
            rows = pl.ds(pl.multiple_of(place * half + start, tile), tile)
            branch = mine_ref[rows, :].astype(f32) + got_ref[rows, :].astype(f32)
            middle = ref[start : start + tile, :].astype(f32) + branch
            middle_ref[rows, :] = middle
            input_ref[rows, :] = (middle * row_factor(middle) * gain_ref[...]).astype(bf16)
            cot_ref[rows, :] = cot[start : start + tile, :]
    pick_ref[...] = picks(index_ref, length)
    ffn_rows = mm(pick_ref[...], input_ref[...], 0, 0)
    rows_ref[...] = ffn_rows.astype(bf16)
    cot_rows_ref[...] = mm(pick_ref[...], cot_ref[...], 0, 0).astype(bf16)
    score = sigmoid(jnp.sum(ffn_rows * route_ref[...], axis=-1, keepdims=True))
    heavy_width = hg_ref.shape[1]
    chunk = 512
    score_grad = 0.0
    down = 0.0
    rows_grad = 0.0
    for start in range(0, heavy_width, chunk):
        cols = slice(start, start + chunk)
        up_cols = slice(heavy_width + start, heavy_width + start + chunk)
        gate = mm(rows_ref[...], hg_ref[:, cols])
        up = mm(rows_ref[...], hu_ref[:, cols])
        act_grad = mm(cot_rows_ref[...], hd_ref[cols, :], 1, 1)
        gelu, slope = gelu_parts(gate)
        mixed = gelu * up
        act_heavy_ref[:, cols] = (score * mixed).astype(bf16)
        score_grad = score_grad + jnp.sum(act_grad * mixed, axis=-1, keepdims=True)
        scaled = score * act_grad
        mix_heavy_ref[:, cols] = (scaled * up * slope).astype(bf16)
        mix_heavy_ref[:, up_cols] = (scaled * gelu).astype(bf16)
        down = down + mm(act_heavy_ref[:, cols], hd_ref[cols, :])
        rows_grad = rows_grad + mm(mix_heavy_ref[:, cols], hg_ref[:, cols], 1, 1)
        rows_grad = rows_grad + mm(mix_heavy_ref[:, up_cols], hu_ref[:, cols], 1, 1)
    logit_grad = score * (1.0 - score) * score_grad
    route_grad_ref[...] = jnp.sum(ffn_rows * logit_grad, axis=0, keepdims=True)
    rows_grad = rows_grad + logit_grad * route_ref[...]
    down_high, down_low = split_low(down)
    back_high, back_low = split_low(rows_grad)
    width = wg_ref.shape[1]
    for first in range(0, 2):
        place = side if first == 0 else 1 - side
        for start in range(0, half, tile):
            rows = pl.ds(pl.multiple_of(place * half + start, tile), tile)
            piece = slice(start, start + tile)
            gate = mm(input_ref[rows, :], wg_ref[...])
            up = mm(input_ref[rows, :], wu_ref[...])
            act_grad = mm(cot_ref[rows, :], wd_ref[...], 1, 1)
            gelu, slope = gelu_parts(gate)
            act_ref[rows, :] = (gelu * up).astype(bf16)
            mix_ref[rows, :width] = (act_grad * up * slope).astype(bf16)
            mix_ref[rows, width:] = (act_grad * gelu).astype(bf16)
            pick = pick_ref[rows, :]
            branch = mm(act_ref[rows, :], wd_ref[...]) + (mm(pick, down_high) + mm(pick, down_low))
            if first == 0:
                block_own_ref[piece, :] = middle_ref[rows, :] + branch
            else:
                block_send_ref[piece, :] = branch.astype(bf16)
            back_ref[rows, :] = (
                mm(mix_ref[rows, :width], wg_ref[...], 1, 1)
                + mm(mix_ref[rows, width:], wu_ref[...], 1, 1)
                + (mm(pick, back_high) + mm(pick, back_low))
            ).astype(bf16)
    light_grad_ref[:, : 2 * width] = mm(input_ref[...], mix_ref[...], 0, 0).astype(bf16)
    light_grad_ref[:, 2 * width :] = mm(cot_ref[...], act_ref[...], 0, 0).astype(bf16)


def attn_backward_kernel(
    own_ref,
    other_ref,
    cot_own_ref,
    cot_other_ref,
    middle_ref,
    mine_ref,
    got_ref,
    gain_attn_ref,
    gain_ffn_ref,
    route_query_ref,
    route_key_ref,
    query_index_ref,
    key_index_ref,
    wq_ref,
    wk_ref,
    wv_ref,
    wo_ref,
    hq_ref,
    hk_ref,
    hv_ref,
    ho_ref,
    input_ref,
    q_ref,
    k_ref,
    v_ref,
    result_ref,
    query_rows_ref,
    key_raw_ref,
    key_rows_ref,
    qh_ref,
    kh_ref,
    vh_ref,
    raw_ref,
    heavy_result_ref,
    own_middle_ref,
    own_back_ref,
    send_ref,
    light_grad_ref,
    out_grad_ref,
    heavy_grad_ref,
    small_ref,
    low_ref,
    out_ref,
    kt_ref,
    qt_grad_ref,
    k_grad_ref,
    v_grad_ref,
    grads_ref,
    pick_ref,
):
    side = lax.axis_index("tensor")
    half = own_ref.shape[0]
    length = 2 * half
    tile = 256
    scale = HEAD_DIM**-0.5
    gain_ffn_grad = 0.0
    for cot, place, owned in ((cot_own_ref, side, True), (cot_other_ref, 1 - side, False)):
        for start in range(0, half, tile):
            rows = pl.ds(pl.multiple_of(place * half + start, tile), tile)
            piece = slice(start, start + tile)
            normed_grad = mine_ref[rows, :].astype(f32) + got_ref[rows, :].astype(f32)
            middle = middle_ref[rows, :]
            factor = row_factor(middle)
            scaled = factor * middle
            gain_ffn_grad = gain_ffn_grad + jnp.sum(scaled * normed_grad, axis=0, keepdims=True)
            gained = gain_ffn_ref[...] * normed_grad
            inner = jnp.mean(scaled * gained, axis=-1, keepdims=True)
            grad = cot[piece, :].astype(f32) + factor * (gained - scaled * inner)
            if owned:
                own_middle_ref[piece, :] = grad
            low_ref[rows, :] = grad.astype(bf16)
    for start in range(0, length, tile):
        rows = slice(start, start + tile)
        out_ref[rows, :] = mm(low_ref[rows, :], wo_ref[...], 1, 1).astype(bf16)
    out_grad_ref[...] = mm(low_ref[...], result_ref[...], 0, 0).astype(bf16)

    routed = query_index_ref.shape[1]
    pick_ref[:, :routed] = picks(query_index_ref, length)
    pick_ref[:, routed:] = picks(key_index_ref, length)
    query_rows = query_rows_ref[...].astype(f32)
    key_raw = key_raw_ref[...].astype(f32)
    query_score = sigmoid(jnp.sum(query_rows * route_query_ref[...], axis=-1, keepdims=True))
    key_score = sigmoid(jnp.sum(key_raw * route_key_ref[...], axis=-1, keepdims=True))
    mid_rows = mm(pick_ref[:, :routed], low_ref[...], 0, 0).astype(bf16)
    heavy = qh_ref.shape[1]
    heavy_grad_ref[:, 3 * heavy :] = mm(mid_rows, heavy_result_ref[...], 0, 0).astype(bf16)
    heavy_out_grad = mm(mid_rows, ho_ref[...], 1, 1).astype(bf16)
    query_score_grad = jnp.sum(
        heavy_out_grad.astype(f32) * raw_ref[...], axis=-1, keepdims=True
    )
    raw_high, raw_low = split_low(query_score * heavy_out_grad.astype(f32))
    pair = 2 * HEAD_DIM
    pair_masks = head_masks(pair)
    stacked_score = jnp.concatenate([query_score] * 2, axis=0)
    q_parts, k_parts, v_parts = [], [], []
    for start in range(0, heavy, pair):
        cols = slice(start, start + pair)
        stacked = stack_heads(qh_ref[:, cols] * scale, pair_masks)
        probs = softmax_rows(mm(stacked, kh_ref[:, cols], 1, 1), -1)
        grad_stacked = stack_heads(heavy_out_grad[:, cols], pair_masks)
        probs_grad = stacked_score * mm(grad_stacked, vh_ref[:, cols], 1, 1)
        inner = jnp.sum(probs * probs_grad, axis=-1, keepdims=True)
        score_grad = (probs * (probs_grad - inner)).astype(bf16)
        probs_low = probs.astype(bf16)
        q_parts.append(unstack_heads(mm(score_grad, kh_ref[:, cols]) * scale, pair_masks))
        k_parts.append(mm(score_grad, stacked, 0, 0))
        v_parts.append(
            mm(probs_low, stack_heads(raw_high[:, cols], pair_masks), 0, 0)
            + mm(probs_low, stack_heads(raw_low[:, cols], pair_masks), 0, 0)
        )
    query_heavy_grad = jnp.concatenate(q_parts, axis=1).astype(bf16)
    key_heavy_grad = jnp.concatenate(k_parts, axis=1).astype(bf16)
    value_heavy_grad = jnp.concatenate(v_parts, axis=1).astype(bf16)
    heavy_grad_ref[:, :heavy] = mm(query_rows_ref[...], query_heavy_grad, 0, 0).astype(bf16)
    heavy_grad_ref[:, heavy : 2 * heavy] = mm(key_rows_ref[...], key_heavy_grad, 0, 0).astype(bf16)
    heavy_grad_ref[:, 2 * heavy : 3 * heavy] = mm(
        key_rows_ref[...], value_heavy_grad, 0, 0
    ).astype(bf16)
    key_rows_grad = mm(key_heavy_grad, hk_ref[...], 1, 1) + mm(
        value_heavy_grad, hv_ref[...], 1, 1
    )
    key_logit_grad = (
        key_score * (1.0 - key_score) * jnp.sum(key_rows_grad * key_raw, axis=-1, keepdims=True)
    )
    query_logit_grad = query_score * (1.0 - query_score) * query_score_grad
    key_raw_grad = key_score * key_rows_grad + key_logit_grad * route_key_ref[...]
    query_rows_grad = mm(query_heavy_grad, hq_ref[...], 1, 1)
    query_rows_grad = query_rows_grad + query_logit_grad * route_query_ref[...]
    small_ref[...] = jnp.zeros_like(small_ref)
    small_ref[1:2, :] = 0.5 * gain_ffn_grad
    small_ref[2:3, :] = jnp.sum(query_rows * query_logit_grad, axis=0, keepdims=True)
    small_ref[3:4, :] = jnp.sum(key_raw * key_logit_grad, axis=0, keepdims=True)
    back_high, back_low = split_low(jnp.concatenate([query_rows_grad, key_raw_grad], axis=0))

    kt_ref[...] = k_ref[...].T
    k_grad_ref[...] = jnp.zeros_like(k_grad_ref)
    v_grad_ref[...] = jnp.zeros_like(v_grad_ref)
    masks = head_masks(q_ref.shape[1])
    heads = len(masks)
    gap = lax.broadcasted_iota(jnp.int32, (3 * WINDOW, WINDOW), 1) - lax.broadcasted_iota(
        jnp.int32, (3 * WINDOW, WINDOW), 0
    )

    def one_block(block, carry):
        first = pl.multiple_of(block * WINDOW, WINDOW)
        rows = pl.ds(first, WINDOW)
        start = window_start(block, length)
        keys = pl.ds(start, 3 * WINDOW)
        stacked = stack_heads(q_ref[rows, :] * scale, masks)
        grad_stacked = stack_heads(out_ref[rows, :], masks)
        near = jnp.abs(gap + (block * WINDOW - start)) < WINDOW
        bias = jnp.where(near, 0.0, -1e30)
        scores = mm(k_ref[keys, :], stacked, 1, 1)
        probs = softmax_rows(scores + jnp.concatenate([bias] * heads, axis=1), 0)
        probs_grad = mm(v_ref[keys, :], grad_stacked, 1, 1)
        inner = jnp.sum(probs * probs_grad, axis=0, keepdims=True)
        score_grad = (probs * (probs_grad - inner)).astype(bf16)
        k_grad_ref[keys, :] += mm(score_grad, stacked)
        v_grad_ref[keys, :] += mm(probs.astype(bf16), grad_stacked)
        spread = mm(kt_ref[:, keys], score_grad) * scale
        for head in range(heads):
            lanes = slice(head * HEAD_DIM, (head + 1) * HEAD_DIM)
            qt_grad_ref[lanes, rows] = spread[lanes, head * WINDOW : (head + 1) * WINDOW]
        return carry

    lax.fori_loop(0, length // WINDOW, one_block, 0)
    light = q_ref.shape[1]
    grads_ref[:, :light] = qt_grad_ref[...].T.astype(bf16)
    grads_ref[:, light : 2 * light] = k_grad_ref[...].astype(bf16)
    grads_ref[:, 2 * light :] = v_grad_ref[...].astype(bf16)
    light_grad_ref[...] = mm(input_ref[...], grads_ref[...], 0, 0).astype(bf16)
    gain_attn_grad = 0.0
    for ref, place, owned in ((own_ref, side, True), (other_ref, 1 - side, False)):
        for start in range(0, half, tile):
            rows = pl.ds(pl.multiple_of(place * half + start, tile), tile)
            piece = slice(start, start + tile)
            pick = pick_ref[rows, :]
            back = (
                mm(grads_ref[rows, :light], wq_ref[...], 1, 1)
                + mm(grads_ref[rows, light : 2 * light], wk_ref[...], 1, 1)
                + mm(grads_ref[rows, 2 * light :], wv_ref[...], 1, 1)
                + (mm(pick, back_high) + mm(pick, back_low))
            )
            values = ref[piece, :].astype(f32)
            gain_attn_grad = gain_attn_grad + jnp.sum(
                values * row_factor(values) * back, axis=0, keepdims=True
            )
            if owned:
                own_back_ref[piece, :] = back
            else:
                send_ref[piece, :] = back.astype(bf16)
    small_ref[0:1, :] = gain_attn_grad


def whole(kernel, name, outs, scratch, *operands):
    return pl.pallas_call(
        kernel,
        name=name,
        out_shape=[jax.ShapeDtypeStruct(shape, dtype) for shape, dtype in outs],
        in_specs=[pl.BlockSpec(memory_space=pltpu.VMEM)] * len(operands),
        out_specs=[pl.BlockSpec(memory_space=pltpu.VMEM)] * len(outs),
        scratch_shapes=[pltpu.VMEM(shape, dtype) for shape, dtype in scratch],
        compiler_params=pltpu.CompilerParams(vmem_limit_bytes=VMEM_LIMIT),
    )(*operands)


def body(
    tokens,
    cotangent,
    gain_attn,
    gain_ffn,
    route_query,
    route_key,
    route_ffn,
    light_query,
    light_key,
    light_value,
    light_out,
    heavy_query,
    heavy_key,
    heavy_value,
    heavy_out,
    light_gate,
    light_up,
    light_down,
    heavy_gate,
    heavy_up,
    heavy_down,
    query_index,
    key_index,
    ffn_index,
):
    half, width = tokens.shape
    length = 2 * half
    routed = query_index.shape[1]
    light = light_query.shape[1]
    heavy = heavy_query.shape[1]
    light_ff = light_gate.shape[1]
    heavy_ff = heavy_gate.shape[1]
    gain_attn, gain_ffn, route_query, route_key, route_ffn = (
        item.reshape(1, -1) for item in (gain_attn, gain_ffn, route_query, route_key, route_ffn)
    )
    other_tokens = pair_swap(tokens)
    other_cotangent = pair_swap(cotangent)
    attn_weights = (
        light_query,
        light_key,
        light_value,
        light_out,
        heavy_query,
        heavy_key,
        heavy_value,
        heavy_out,
    )
    attn_partial, *saved = whole(
        attn_forward_kernel,
        "attn_forward",
        [((length, width), bf16)] * 2
        + [((length, light), bf16)] * 4
        + [((routed, width), bf16)] * 3
        + [((routed, heavy), bf16)] * 3
        + [((routed, heavy), f32), ((routed, heavy), bf16)],
        [((length, 2 * routed), bf16)],
        tokens,
        other_tokens,
        gain_attn,
        route_query,
        route_key,
        query_index,
        key_index,
        *attn_weights,
    )
    (
        middle,
        block_own,
        block_send,
        ffn_back,
        light_ffn_grad,
        ffn_rows,
        cot_rows,
        act_heavy,
        mix_heavy,
        route_ffn_grad,
    ) = whole(
        ffn_kernel,
        "ffn",
        [
            ((length, width), f32),
            ((half, width), f32),
            ((half, width), bf16),
            ((length, width), bf16),
            ((width, 3 * light_ff), bf16),
            ((routed, width), bf16),
            ((routed, width), bf16),
            ((routed, heavy_ff), bf16),
            ((routed, 2 * heavy_ff), bf16),
            ((1, width), f32),
        ],
        [
            ((length, width), bf16),
            ((length, width), bf16),
            ((length, light_ff), bf16),
            ((length, 2 * light_ff), bf16),
            ((length, routed), bf16),
        ],
        tokens,
        other_tokens,
        attn_partial,
        pair_swap(attn_partial),
        cotangent,
        other_cotangent,
        gain_ffn,
        route_ffn,
        ffn_index,
        light_gate,
        light_up,
        light_down,
        heavy_gate,
        heavy_up,
        heavy_down,
    )
    block_out = (block_own + pair_swap(block_send).astype(f32)).astype(bf16)
    own_middle, own_back, back_send, light_grad, out_grad, heavy_grad, small = whole(
        attn_backward_kernel,
        "attn_backward",
        [
            ((half, width), f32),
            ((half, width), f32),
            ((half, width), bf16),
            ((width, 3 * light), bf16),
            ((width, light), bf16),
            ((width, 4 * heavy), bf16),
            ((8, width), f32),
        ],
        [
            ((length, width), bf16),
            ((length, light), bf16),
            ((light, length), bf16),
            ((light, length), f32),
            ((length, light), f32),
            ((length, light), f32),
            ((length, 3 * light), bf16),
            ((length, 2 * routed), bf16),
        ],
        tokens,
        other_tokens,
        cotangent,
        other_cotangent,
        middle,
        ffn_back,
        pair_swap(ffn_back),
        gain_attn,
        gain_ffn,
        route_query,
        route_key,
        query_index,
        key_index,
        *attn_weights,
        *saved,
    )
    normed_grad = own_back + pair_swap(back_send).astype(f32)
    own_tokens = tokens.astype(f32)
    factor = row_factor(own_tokens)
    scaled = own_tokens * factor
    gained = gain_attn * normed_grad
    inner = jnp.mean(scaled * gained, axis=-1, keepdims=True)
    input_grad = (own_middle + factor * (gained - scaled * inner)).astype(bf16)
    small_summed = butterfly_sum(small + jnp.pad(route_ffn_grad, ((4, 3), (0, 0))))

    forward_order = list(range(lax.axis_size("dp").bit_length() - 1))
    other_order = [1, 0] + forward_order[2:]
    heavy_mix_grad = mm(ffn_rows, mix_heavy, 0, 0).astype(bf16)
    heavy_down_grad = mm(cot_rows, act_heavy, 0, 0).astype(bf16)
    mixed_sum = halving_sum(heavy_mix_grad, forward_order)
    down_sum = halving_sum(heavy_down_grad, other_order)
    light_ffn_sum = halving_sum(light_ffn_grad, other_order)
    heavy_sum = halving_sum(heavy_grad, forward_order)
    light_sum = halving_sum(light_grad, other_order)
    out_sum = halving_sum(out_grad, other_order)
    return (
        block_out,
        input_grad,
        small_summed[0],
        small_summed[1],
        small_summed[2],
        small_summed[3],
        small_summed[4],
        light_sum[:, :light],
        light_sum[:, light : 2 * light],
        light_sum[:, 2 * light :],
        out_sum.T,
        heavy_sum[:, :heavy],
        heavy_sum[:, heavy : 2 * heavy],
        heavy_sum[:, 2 * heavy : 3 * heavy],
        heavy_sum[:, 3 * heavy :].T,
        light_ffn_sum[:, :light_ff],
        light_ffn_sum[:, light_ff : 2 * light_ff],
        light_ffn_sum[:, 2 * light_ff :].T,
        mixed_sum[:, :heavy_ff],
        mixed_sum[:, heavy_ff:],
        down_sum.T,
    )


def solution(mesh):
    in_specs = (
        P(("dp", "tensor"), None),
        P(("dp", "tensor"), None),
        P(),
        P(),
        P(),
        P(),
        P(),
        P(None, "tensor"),
        P(None, "tensor"),
        P(None, "tensor"),
        P("tensor", None),
        P(None, "tensor"),
        P(None, "tensor"),
        P(None, "tensor"),
        P("tensor", None),
        P(None, "tensor"),
        P(None, "tensor"),
        P("tensor", None),
        P(None, "tensor"),
        P(None, "tensor"),
        P("tensor", None),
        P("dp", None),
        P("dp", None),
        P("dp", None),
    )
    out_specs = (
        P(("dp", "tensor"), None),
        P(("dp", "tensor"), None),
        P(),
        P(),
        P(),
        P(),
        P(),
        P("dp", "tensor"),
        P("dp", "tensor"),
        P("dp", "tensor"),
        P("tensor", "dp"),
        P("dp", "tensor"),
        P("dp", "tensor"),
        P("dp", "tensor"),
        P("tensor", "dp"),
        P("dp", "tensor"),
        P("dp", "tensor"),
        P("tensor", "dp"),
        P("dp", "tensor"),
        P("dp", "tensor"),
        P("tensor", "dp"),
    )
    return jax.shard_map(body, mesh=mesh, in_specs=in_specs, out_specs=out_specs, check_vma=False)
```

profile of v0, /device:TPU:0, one launch (start us, length us, event | category | flops | bytes accessed | tf_op | source)
XLA Modules:
  0.0 306.3 jit_solution(2398789323269012226)
XLA Ops:
  5.9 16.1 %attn_forward.1 = (bf16[1024,768]{1,0:T(8,128)(2,1)}, bf16[1024,768]{1,0:T(8,128)(2,1)}, bf16[1024,256]{1,0:T(8,128)(2,1)}, bf16[1024,256]{1,0:T(8,128)(2,1)}, b...) custom-call(bf16[512,768]{1,0:T(8,128)(2,1)} %own_ref.5, ...), custom_call_target="tpu_custom_call" | custom-call | tf_op jit(solution)/shard_map/attn_forward/pallas_call | solution.py:503
  24.0 2.4 collective-permute-done.2.cot_other_ref
  27.2 24.0 %ffn.1 = (f32[1024,768]{1,0:T(8,128)}, f32[512,768]{1,0:T(8,128)}, bf16[512,768]{1,0:T(8,128)(2,1)}, bf16[1024,768]{1,0:T(8,128)(2,1)}, bf16[768,1536]{1,0:T(8,1...) custom-call(bf16[512,768]{1,0:T(8,128)(2,1)} %own_ref.5, ...), custom_call_target="tpu_custom_call" | custom-call | tf_op jit(solution)/shard_map/ffn/pallas_call | solution.py:503
  53.8 2.8 collective-permute-start.23
  68.5 14.9 %collective-permute-done.23 = bf16[2,2,2,48,1536]{4,3,0,1,2:T(8,128)(2,1)S(1)} collective-permute-done((bf16[2,2,2,48,1536]{4,3,0,1,2:T(8,128)(2,1)S(1)}, bf16[2,2,2,48,1536]{4,3,0,1,2:T(8,128)(2,1)S(1)}, u32[]{:S(2)}, u32[]{:S(2)}) %collective-permute-start.23) | collective-permute-done | bytes 1179680 | tf_op jit(solution)/shard_map/ppermute | solution.py:32
  87.0 25.6 %attn_backward.1 = (f32[512,768]{1,0:T(8,128)}, f32[512,768]{1,0:T(8,128)}, bf16[512,768]{1,0:T(8,128)(2,1)}, bf16[768,768]{1,0:T(8,128)(2,1)}, bf16[768,256]{1,...) custom-call(bf16[512,768]{1,0:T(8,128)(2,1)} %own_ref.5, bf16[512,768]{1,0:T(8,128)(2,1)} %copy-done.2, ...), custom_call_target="tpu_custom_call" | custom-call | tf_op jit(solution)/shard_map/attn_backward/pallas_call | solution.py:503
  118.9 2.6 fusion.1
  121.5 22.8 %collective-permute-done.7 = f32[8,768]{1,0:T(8,128)S(1)} collective-permute-done((f32[8,768]{1,0:T(8,128)S(1)}, f32[8,768]{1,0:T(8,128)S(1)}, u32[]{:S(2)}, u32[]{:S(2)}) %collective-permute-start.7) | collective-permute-done | bytes 24608 | tf_op jit(solution)/shard_map/ppermute | solution.py:43
  152.0 2.6 collective-permute-start.10
  167.1 3.0 collective-permute-start.18
  175.0 2.8 collective-permute-start.26
  177.9 3.2 %collective-permute-done.26 = bf16[48,1536]{1,0:T(8,128)(2,1)S(1)} collective-permute-done((bf16[48,1536]{1,0:T(8,128)(2,1)S(1)}, bf16[48,1536]{1,0:T(8,128)(2,1)S(1)}, u32[]{:S(2)}, u32[]{:S(2)}) %collective-permute-start.26) | collective-permute-done | bytes 147488 | tf_op jit(solution)/shard_map/ppermute | solution.py:32
  183.4 29.3 %collective-permute-done.32 = bf16[2,2,48,2048]{3,2,0,1:T(8,128)(2,1)S(1)} collective-permute-done((bf16[2,2,48,2048]{3,2,0,1:T(8,128)(2,1)S(1)}, bf16[2,2,48,2048]{3,2,0,1:T(8,128)(2,1)S(1)}, u32[]{:S(2)}, u32[]{:S(2)}) %collective-permute-start.32) | collective-permute-done | bytes 786464 | tf_op jit(solution)/shard_map/ppermute | solution.py:32
  213.5 2.3 collective-permute-done.12
  215.9 2.9 collective-permute-start.13
  219.0 3.0 collective-permute-done.13
  225.1 2.8 collective-permute-done.14
  228.9 3.1 %fusion = bf16[2,2,2,48,4096]{4,3,0,1,2:T(8,128)(2,1)S(1)} fusion(bf16[2,2,2,48,4096]{4,3,0,1,2:T(8,128)(2,1)} %collective-permute-done.27, bf16[2,2,2,1,48,4096]{5,4,3,2,1,0:T(8,128)(2,1)S(1)} %get-tuple-element.88), kind=kLoop, calls=%fused_computation.2 | loop fusion | flops 6291456 | bytes 9437184 | tf_op jit(solution)/shard_map/convert_element_type | solution.py:35
  234.5 2.4 collective-permute-start.34
  236.9 33.4 %collective-permute-done.20 = bf16[2,2,48,1536]{3,2,0,1:T(8,128)(2,1)S(1)} collective-permute-done((bf16[2,2,48,1536]{3,2,0,1:T(8,128)(2,1)S(1)}, bf16[2,2,48,1536]{3,2,0,1:T(8,128)(2,1)S(1)}, u32[]{:S(2)}, u32[]{:S(2)}) %collective-permute-start.20) | collective-permute-done | bytes 589856 | tf_op jit(solution)/shard_map/ppermute | solution.py:32
  274.1 3.6 %collective-permute-done.21 = bf16[2,48,1536]{2,1,0:T(8,128)(2,1)S(1)} collective-permute-done((bf16[2,48,1536]{2,1,0:T(8,128)(2,1)S(1)}, bf16[2,48,1536]{2,1,0:T(8,128)(2,1)S(1)}, u32[]{:S(2)}, u32[]{:S(2)}) %collective-permute-start.21) | collective-permute-done | bytes 294944 | tf_op jit(solution)/shard_map/ppermute | solution.py:32
  277.8 4.0 %collective-permute-start.22 = (bf16[48,1536]{1,0:T(8,128)(2,1)S(1)}, bf16[48,1536]{1,0:T(8,128)(2,1)S(1)}, u32[]{:S(2)}, u32[]{:S(2)}) collective-permute-start(bf16[48,1536]{1,0:T(8,128)(2,1)S(1)} %dynamic-slice_bitcast_fusion.12), channel_id=1, source_target_pairs={{0,16},{2,18},{4,20},{6,22},{8,24},{10,26},{12,28},{14,30},{16,0},... | collective-permute-start | bytes 442376 | tf_op jit(solution)/shard_map/ppermute | solution.py:32
  281.8 10.1 %collective-permute-done.29 = bf16[2,48,4096]{2,1,0:T(8,128)(2,1)S(1)} collective-permute-done((bf16[2,48,4096]{2,1,0:T(8,128)(2,1)S(1)}, bf16[2,48,4096]{2,1,0:T(8,128)(2,1)S(1)}, u32[]{:S(2)}, u32[]{:S(2)}) %collective-permute-start.29) | collective-permute-done | bytes 786464 | tf_op jit(solution)/shard_map/ppermute | solution.py:32
  295.1 10.0 %collective-permute-done.30 = bf16[48,4096]{1,0:T(8,128)(2,1)S(1)} collective-permute-done((bf16[48,4096]{1,0:T(8,128)(2,1)S(1)}, bf16[48,4096]{1,0:T(8,128)(2,1)S(1)}, u32[]{:S(2)}, u32[]{:S(2)}) %collective-permute-start.30) | collective-permute-done | bytes 393248 | tf_op jit(solution)/shard_map/ppermute | solution.py:32
  (167 shorter events, 75.2 us)
Async XLA Ops:
  51.2 16.2 %collective-permute-start.3 = (bf16[512,768]{1,0:T(8,128)(2,1)}, bf16[512,768]{1,0:T(8,128)(2,1)S(1)}, u32[]{:S(2)}, u32[]{:S(2)}) collective-permute-start(bf16[512,768]{1,0:T(8,128)(2,1)} %get-tuple-element.54), channel_id=1, source_target_pairs={{0,1},{1,0},{2,3},{3,2},{4,5},{5,4},{6,7},{7,6},{8,9},{9,8},{10,11... | collective-permute-start | bytes 2359304 | tf_op jit(solution)/shard_map/ppermute | solution.py:17
  51.6 35.3 %collective-permute-start.4 = (bf16[1024,768]{1,0:T(8,128)(2,1)}, bf16[1024,768]{1,0:T(8,128)(2,1)}, u32[]{:S(2)}, u32[]{:S(2)}) collective-permute-start(bf16[1024,768]{1,0:T(8,128)(2,1)} %get-tuple-element.56.mine_ref), channel_id=1, source_target_pairs={{0,1},{1,0},{2,3},{3,2},{4,5},{5,4},{6,7},{7,6},{8,9},{9,8},{10,11... | collective-permute-start | bytes 4718600 | tf_op jit(solution)/shard_map/ppermute | solution.py:17
  53.8 29.6 %collective-permute-start.23 = (bf16[2,2,2,48,1536]{4,3,0,1,2:T(8,128)(2,1)S(1)}, bf16[2,2,2,48,1536]{4,3,0,1,2:T(8,128)(2,1)S(1)}, u32[]{:S(2)}, u32[]{:S(2)}) collective-permute-start(bf16[2,2,2,48,1536]{4,3,0,1,2:T(8,128)(2,1)S(1)} %bitcast.162), channel_id=1, source_target_pairs={{0,4},{2,6},{4,0},{6,2},{8,12},{10,14},{12,8},{14,10},{16,20},{18,... | collective-permute-start | bytes 3538952 | tf_op jit(solution)/shard_map/ppermute | solution.py:32
  61.0 168.0 %collective-permute-start.27 = (bf16[2,2,2,48,4096]{4,3,0,1,2:T(8,128)(2,1)}, bf16[2,2,2,48,4096]{4,3,0,1,2:T(8,128)(2,1)}, u32[]{:S(2)}, u32[]{:S(2)}) collective-permute-start(bf16[2,2,2,48,4096]{4,3,0,1,2:T(8,128)(2,1)} %bitcast.150), channel_id=1, source_target_pairs={{0,2},{2,0},{4,6},{6,4},{8,10},{10,8},{12,14},{14,12},{16,18},{18,... | collective-permute-start | bytes 9437192 | tf_op jit(solution)/shard_map/ppermute | solution.py:32
  66.4 51.1 %collective-permute-start.31 = (bf16[2,2,2,48,2048]{4,3,0,1,2:T(8,128)(2,1)}, bf16[2,2,2,48,2048]{4,3,0,1,2:T(8,128)(2,1)}, u32[]{:S(2)}, u32[]{:S(2)}) collective-permute-start(bf16[2,2,2,48,2048]{4,3,0,1,2:T(8,128)(2,1)} %bitcast.151), channel_id=1, source_target_pairs={{0,4},{2,6},{4,0},{6,2},{8,12},{10,14},{12,8},{14,10},{16,20},{18,... | collective-permute-start | bytes 4718600 | tf_op jit(solution)/shard_map/ppermute | solution.py:32
  84.9 74.9 %collective-permute-start.24 = (bf16[2,2,48,1536]{3,2,0,1:T(8,128)(2,1)S(1)}, bf16[2,2,48,1536]{3,2,0,1:T(8,128)(2,1)}, u32[]{:S(2)}, u32[]{:S(2)}) collective-permute-start(bf16[2,2,48,1536]{3,2,0,1:T(8,128)(2,1)S(1)} %dynamic-slice_bitcast_fusion.3), channel_id=1, source_target_pairs={{0,2},{2,0},{4,6},{6,4},{8,10},{10,8},{12,14},{14,12},{16,18},{18,... | collective-permute-start | bytes 1769480 | tf_op jit(solution)/shard_map/ppermute | solution.py:32
  112.6 100.4 %collective-permute-start.5 = (bf16[512,768]{1,0:T(8,128)(2,1)}, bf16[512,768]{1,0:T(8,128)(2,1)S(1)}, u32[]{:S(2)}, u32[]{:S(2)}) collective-permute-start(bf16[512,768]{1,0:T(8,128)(2,1)} %get-tuple-element.72), channel_id=1, source_target_pairs={{0,1},{1,0},{2,3},{3,2},{4,5},{5,4},{6,7},{7,6},{8,9},{9,8},{10,11... | collective-permute-start | bytes 2359304 | tf_op jit(solution)/shard_map/ppermute | solution.py:17
  115.1 43.0 %collective-permute-start.15 = (bf16[2,2,2,48,256]{4,3,0,1,2:T(8,128)(2,1)S(1)}, bf16[2,2,2,48,256]{4,3,0,1,2:T(8,128)(2,1)S(1)}, u32[]{:S(2)}, u32[]{:S(2)}) collective-permute-start(bf16[2,2,2,48,256]{4,3,0,1,2:T(8,128)(2,1)S(1)} %bitcast.165), channel_id=1, source_target_pairs={{0,4},{2,6},{4,0},{6,2},{8,12},{10,14},{12,8},{14,10},{16,20},{18,... | collective-permute-start | bytes 589832 | tf_op jit(solution)/shard_map/ppermute | solution.py:32
  117.4 26.9 %collective-permute-start.7 = (f32[8,768]{1,0:T(8,128)S(1)}, f32[8,768]{1,0:T(8,128)S(1)}, u32[]{:S(2)}, u32[]{:S(2)}) collective-permute-start(f32[8,768]{1,0:T(8,128)S(1)} %fusion.34), channel_id=1, source_target_pairs={{0,2},{2,0},{4,6},{6,4},{8,10},{10,8},{12,14},{14,12},{16,18},{18,... | collective-permute-start | bytes 73736 | tf_op jit(solution)/shard_map/ppermute | solution.py:43
  156.8 18.2 %collective-permute-start.11 = (bf16[2,2,2,48,768]{4,3,0,1,2:T(8,128)(2,1)S(1)}, bf16[2,2,2,48,768]{4,3,0,1,2:T(8,128)(2,1)S(1)}, u32[]{:S(2)}, u32[]{:S(2)}) collective-permute-start(bf16[2,2,2,48,768]{4,3,0,1,2:T(8,128)(2,1)S(1)} %bitcast.163), channel_id=1, source_target_pairs={{0,4},{2,6},{4,0},{6,2},{8,12},{10,14},{12,8},{14,10},{16,20},{18,... | collective-permute-start | bytes 1769480 | tf_op jit(solution)/shard_map/ppermute | solution.py:32
  164.6 9.8 %collective-permute-start.25 = (bf16[2,48,1536]{2,1,0:T(8,128)(2,1)S(1)}, bf16[2,48,1536]{2,1,0:T(8,128)(2,1)S(1)}, u32[]{:S(2)}, u32[]{:S(2)}) collective-permute-start(bf16[2,48,1536]{2,1,0:T(8,128)(2,1)S(1)} %dynamic-slice_bitcast_fusion.7), channel_id=1, source_target_pairs={{0,8},{2,10},{4,12},{6,14},{8,0},{10,2},{12,4},{14,6},{16,24},{18,... | collective-permute-start | bytes 884744 | tf_op jit(solution)/shard_map/ppermute | solution.py:32
  172.2 56.4 %collective-permute-start.19 = (bf16[2,2,2,48,1536]{4,3,0,1,2:T(8,128)(2,1)S(1)}, bf16[2,2,2,48,1536]{4,3,0,1,2:T(8,128)(2,1)S(1)}, u32[]{:S(2)}, u32[]{:S(2)}) collective-permute-start(bf16[2,2,2,48,1536]{4,3,0,1,2:T(8,128)(2,1)S(1)} %bitcast.160), channel_id=1, source_target_pairs={{0,2},{2,0},{4,6},{6,4},{8,10},{10,8},{12,14},{14,12},{16,18},{18,... | collective-permute-start | bytes 3538952 | tf_op jit(solution)/shard_map/ppermute | solution.py:32
  174.3 38.3 %collective-permute-start.32 = (bf16[2,2,48,2048]{3,2,0,1:T(8,128)(2,1)S(1)}, bf16[2,2,48,2048]{3,2,0,1:T(8,128)(2,1)S(1)}, u32[]{:S(2)}, u32[]{:S(2)}) collective-permute-start(bf16[2,2,48,2048]{3,2,0,1:T(8,128)(2,1)S(1)} %dynamic-slice_bitcast_fusion.1), channel_id=1, source_target_pairs={{0,2},{2,0},{4,6},{6,4},{8,10},{10,8},{12,14},{14,12},{16,18},{18,... | collective-permute-start | bytes 2359304 | tf_op jit(solution)/shard_map/ppermute | solution.py:32
  175.0 6.1 %collective-permute-start.26 = (bf16[48,1536]{1,0:T(8,128)(2,1)S(1)}, bf16[48,1536]{1,0:T(8,128)(2,1)S(1)}, u32[]{:S(2)}, u32[]{:S(2)}) collective-permute-start(bf16[48,1536]{1,0:T(8,128)(2,1)S(1)} %dynamic-slice_bitcast_fusion.11), channel_id=1, source_target_pairs={{0,16},{2,18},{4,20},{6,22},{8,24},{10,26},{12,28},{14,30},{16,0},... | collective-permute-start | bytes 442376 | tf_op jit(solution)/shard_map/ppermute | solution.py:32
  181.1 34.7 %collective-permute-start.12 = (bf16[2,2,48,768]{3,2,0,1:T(8,128)(2,1)S(1)}, bf16[2,2,48,768]{3,2,0,1:T(8,128)(2,1)S(1)}, u32[]{:S(2)}, u32[]{:S(2)}) collective-permute-start(bf16[2,2,48,768]{3,2,0,1:T(8,128)(2,1)S(1)} %dynamic-slice_bitcast_fusion.9), channel_id=1, source_target_pairs={{0,2},{2,0},{4,6},{6,4},{8,10},{10,8},{12,14},{14,12},{16,18},{18,... | collective-permute-start | bytes 884744 | tf_op jit(solution)/shard_map/ppermute | solution.py:32
  215.9 6.1 %collective-permute-start.13 = (bf16[2,48,768]{2,1,0:T(8,128)(2,1)S(1)}, bf16[2,48,768]{2,1,0:T(8,128)(2,1)S(1)}, u32[]{:S(2)}, u32[]{:S(2)}) collective-permute-start(bf16[2,48,768]{2,1,0:T(8,128)(2,1)S(1)} %dynamic-slice_bitcast_fusion.13), channel_id=1, source_target_pairs={{0,8},{2,10},{4,12},{6,14},{8,0},{10,2},{12,4},{14,6},{16,24},{18,... | collective-permute-start | bytes 442376 | tf_op jit(solution)/shard_map/ppermute | solution.py:32
  218.9 15.5 %collective-permute-start.33 = (bf16[2,48,2048]{2,1,0:T(8,128)(2,1)S(1)}, bf16[2,48,2048]{2,1,0:T(8,128)(2,1)S(1)}, u32[]{:S(2)}, u32[]{:S(2)}) collective-permute-start(bf16[2,48,2048]{2,1,0:T(8,128)(2,1)S(1)} %dynamic-slice_bitcast_fusion.5), channel_id=1, source_target_pairs={{0,8},{2,10},{4,12},{6,14},{8,0},{10,2},{12,4},{14,6},{16,24},{18,... | collective-permute-start | bytes 1179656 | tf_op jit(solution)/shard_map/ppermute | solution.py:32
  232.2 40.2 %collective-permute-start.28 = (bf16[2,2,48,4096]{3,2,0,1:T(8,128)(2,1)S(1)}, bf16[2,2,48,4096]{3,2,0,1:T(8,128)(2,1)S(1)}, u32[]{:S(2)}, u32[]{:S(2)}) collective-permute-start(bf16[2,2,48,4096]{3,2,0,1:T(8,128)(2,1)S(1)} %dynamic-slice_bitcast_fusion), channel_id=1, source_target_pairs={{0,4},{2,6},{4,0},{6,2},{8,12},{10,14},{12,8},{14,10},{16,20},{18,... | collective-permute-start | bytes 4718600 | tf_op jit(solution)/shard_map/ppermute | solution.py:32
  232.8 37.5 %collective-permute-start.20 = (bf16[2,2,48,1536]{3,2,0,1:T(8,128)(2,1)S(1)}, bf16[2,2,48,1536]{3,2,0,1:T(8,128)(2,1)S(1)}, u32[]{:S(2)}, u32[]{:S(2)}) collective-permute-start(bf16[2,2,48,1536]{3,2,0,1:T(8,128)(2,1)S(1)} %dynamic-slice_bitcast_fusion.4), channel_id=1, source_target_pairs={{0,4},{2,6},{4,0},{6,2},{8,12},{10,14},{12,8},{14,10},{16,20},{18,... | collective-permute-start | bytes 1769480 | tf_op jit(solution)/shard_map/ppermute | solution.py:32
  234.5 38.8 %collective-permute-start.34 = (bf16[48,2048]{1,0:T(8,128)(2,1)S(1)}, bf16[48,2048]{1,0:T(8,128)(2,1)S(1)}, u32[]{:S(2)}, u32[]{:S(2)}) collective-permute-start(bf16[48,2048]{1,0:T(8,128)(2,1)S(1)} %dynamic-slice_bitcast_fusion.10), channel_id=1, source_target_pairs={{0,16},{2,18},{4,20},{6,22},{8,24},{10,26},{12,28},{14,30},{16,0},... | collective-permute-start | bytes 589832 | tf_op jit(solution)/shard_map/ppermute | solution.py:32
  270.5 7.2 %collective-permute-start.21 = (bf16[2,48,1536]{2,1,0:T(8,128)(2,1)S(1)}, bf16[2,48,1536]{2,1,0:T(8,128)(2,1)S(1)}, u32[]{:S(2)}, u32[]{:S(2)}) collective-permute-start(bf16[2,48,1536]{2,1,0:T(8,128)(2,1)S(1)} %dynamic-slice_bitcast_fusion.8), channel_id=1, source_target_pairs={{0,8},{2,10},{4,12},{6,14},{8,0},{10,2},{12,4},{14,6},{16,24},{18,... | collective-permute-start | bytes 884744 | tf_op jit(solution)/shard_map/ppermute | solution.py:32
  273.0 18.9 %collective-permute-start.29 = (bf16[2,48,4096]{2,1,0:T(8,128)(2,1)S(1)}, bf16[2,48,4096]{2,1,0:T(8,128)(2,1)S(1)}, u32[]{:S(2)}, u32[]{:S(2)}) collective-permute-start(bf16[2,48,4096]{2,1,0:T(8,128)(2,1)S(1)} %dynamic-slice_bitcast_fusion.2), channel_id=1, source_target_pairs={{0,8},{2,10},{4,12},{6,14},{8,0},{10,2},{12,4},{14,6},{16,24},{18,... | collective-permute-start | bytes 2359304 | tf_op jit(solution)/shard_map/ppermute | solution.py:32
  277.8 16.5 %collective-permute-start.22 = (bf16[48,1536]{1,0:T(8,128)(2,1)S(1)}, bf16[48,1536]{1,0:T(8,128)(2,1)S(1)}, u32[]{:S(2)}, u32[]{:S(2)}) collective-permute-start(bf16[48,1536]{1,0:T(8,128)(2,1)S(1)} %dynamic-slice_bitcast_fusion.12), channel_id=1, source_target_pairs={{0,16},{2,18},{4,20},{6,22},{8,24},{10,26},{12,28},{14,30},{16,0},... | collective-permute-start | bytes 442376 | tf_op jit(solution)/shard_map/ppermute | solution.py:32
  292.1 13.0 %collective-permute-start.30 = (bf16[48,4096]{1,0:T(8,128)(2,1)S(1)}, bf16[48,4096]{1,0:T(8,128)(2,1)S(1)}, u32[]{:S(2)}, u32[]{:S(2)}) collective-permute-start(bf16[48,4096]{1,0:T(8,128)(2,1)S(1)} %dynamic-slice_bitcast_fusion.6), channel_id=1, source_target_pairs={{0,16},{2,18},{4,20},{6,22},{8,24},{10,26},{12,28},{14,30},{16,0},... | collective-permute-start | bytes 1179656 | tf_op jit(solution)/shard_map/ppermute | solution.py:32
  (31 other events, 302.3 us)
where the time goes:
time: 310 us; the launch traced here: 306 us
  waiting for transfers between devices  150 us (48%)
  Pallas kernels  65.7 us (21%)
  starting transfers between devices  50.1 us (16%)
  local copies, waits for them, and re-layouts  20.4 us (7%)
  other arithmetic  15.7 us (5%)
    ppermute x24, waiting for transfers between devices, halving_sum(): got = lax.ppermute(send, 'dp', [(i, i ^ 1 << bit) for i in range(parts)])  118 us
    pallas_call x3, Pallas kernels, whole(): pl.pallas_call(kernel, name=name, out_shape=[jax.ShapeDtypeStruct(shape,...  65.7 us
    ppermute x24, starting transfers between devices, halving_sum(): got = lax.ppermute(send, 'dp', [(i, i ^ 1 << bit) for i in range(parts)])  40.9 us
    ppermute x4, waiting for transfers between devices, butterfly_sum(): lax.ppermute(values, 'dp', [(i, i ^ 1 << bit) for i in range(parts)])  29.2 us
    convert_element_type x18, other arithmetic, halving_sum(): held = held.astype(jnp.bfloat16)  9.36 us
    ppermute x4, starting transfers between devices, butterfly_sum(): lax.ppermute(values, 'dp', [(i, i ^ 1 << bit) for i in range(parts)])  6.96 us
  transfers between devices with their start and end apart: 35, of which 19 were waited for; matrix products, arithmetic and copies ran while one was open for 12% of the time, Pallas kernels for 8%

commit v1 on v0

--- a/solution.py
+++ b/solution.py
@@ -1,3 +1,5 @@
+import functools
+
 import jax
 import jax.numpy as jnp
 from jax import lax
@@ -42,6 +44,33 @@
     for bit in range(parts.bit_length() - 1):
         values = values + lax.ppermute(values, "dp", [(i, i ^ (1 << bit)) for i in range(parts)])
     return values
+
+
+PARTS = 16
+LANES = ((0, 1, 2, 3), (1, 2, 0, 3), (2, 0, 1, 3))
+RIDES = (1, 2, 0)
+
+
+def insert(number, bit, value):
+    low = number & ((1 << bit) - 1)
+    return ((number - low) << 1) | (value << bit) | low
+
+
+def after(token, values):
+    return lax.optimization_barrier((values, token))[0]
+
+
+def block_rows(index, block):
+    return pl.ds(pl.multiple_of(index * block, 16), block)
+
+
+def swap_bit(values, bit):
+    parts = lax.axis_size("dp")
+    return lax.ppermute(values, "dp", [(i, i ^ (1 << bit)) for i in range(parts)])
+
+
+def my_bit(bit):
+    return lax.shift_right_logical(lax.axis_index("dp"), bit) & 1
 
 
 def mm(left, right, left_dim=1, right_dim=0):
@@ -201,7 +230,7 @@
     return values * below, below + values * density
 
 
-def ffn_kernel(
+def ffn_heavy_kernel(
     own_ref,
     other_ref,
     mine_ref,
@@ -211,27 +240,19 @@
     gain_ref,
     route_ref,
     index_ref,
-    wg_ref,
-    wu_ref,
-    wd_ref,
     hg_ref,
     hu_ref,
     hd_ref,
+    send_x_ref,
+    send_y_ref,
+    send_z_ref,
     middle_ref,
-    block_own_ref,
-    block_send_ref,
-    back_ref,
-    light_grad_ref,
-    rows_ref,
-    cot_rows_ref,
-    act_heavy_ref,
-    mix_heavy_ref,
-    route_grad_ref,
     input_ref,
     cot_ref,
-    act_ref,
-    mix_ref,
     pick_ref,
+    down_ref,
+    back_ref,
+    route_grad_ref,
 ):
     side = lax.axis_index("tensor")
     half = own_ref.shape[0]
@@ -247,8 +268,12 @@
             cot_ref[rows, :] = cot[start : start + tile, :]
     pick_ref[...] = picks(index_ref, length)
     ffn_rows = mm(pick_ref[...], input_ref[...], 0, 0)
-    rows_ref[...] = ffn_rows.astype(bf16)
-    cot_rows_ref[...] = mm(pick_ref[...], cot_ref[...], 0, 0).astype(bf16)
+    rows_low = ffn_rows.astype(bf16)
+    cot_rows = mm(pick_ref[...], cot_ref[...], 0, 0).astype(bf16)
+    routed, model = rows_low.shape
+    send_x_ref[:, :model] = rows_low
+    send_y_ref[:, :model] = rows_low
+    send_z_ref[:, :model] = cot_rows
     score = sigmoid(jnp.sum(ffn_rows * route_ref[...], axis=-1, keepdims=True))
     heavy_width = hg_ref.shape[1]
     chunk = 512
@@ -257,25 +282,50 @@
     rows_grad = 0.0
     for start in range(0, heavy_width, chunk):
         cols = slice(start, start + chunk)
-        up_cols = slice(heavy_width + start, heavy_width + start + chunk)
-        gate = mm(rows_ref[...], hg_ref[:, cols])
-        up = mm(rows_ref[...], hu_ref[:, cols])
-        act_grad = mm(cot_rows_ref[...], hd_ref[cols, :], 1, 1)
+        out_cols = slice(model + start, model + start + chunk)
+        gate = mm(rows_low, hg_ref[:, cols])
+        up = mm(rows_low, hu_ref[:, cols])
+        act_grad = mm(cot_rows, hd_ref[cols, :], 1, 1)
         gelu, slope = gelu_parts(gate)
         mixed = gelu * up
-        act_heavy_ref[:, cols] = (score * mixed).astype(bf16)
         score_grad = score_grad + jnp.sum(act_grad * mixed, axis=-1, keepdims=True)
         scaled = score * act_grad
-        mix_heavy_ref[:, cols] = (scaled * up * slope).astype(bf16)
-        mix_heavy_ref[:, up_cols] = (scaled * gelu).astype(bf16)
-        down = down + mm(act_heavy_ref[:, cols], hd_ref[cols, :])
-        rows_grad = rows_grad + mm(mix_heavy_ref[:, cols], hg_ref[:, cols], 1, 1)
-        rows_grad = rows_grad + mm(mix_heavy_ref[:, up_cols], hu_ref[:, cols], 1, 1)
+        act = (score * mixed).astype(bf16)
+        gate_grad = (scaled * up * slope).astype(bf16)
+        up_grad = (scaled * gelu).astype(bf16)
+        send_x_ref[:, out_cols] = gate_grad
+        send_y_ref[:, out_cols] = up_grad
+        send_z_ref[:, out_cols] = act
+        down = down + mm(act, hd_ref[cols, :])
+        rows_grad = rows_grad + mm(gate_grad, hg_ref[:, cols], 1, 1)
+        rows_grad = rows_grad + mm(up_grad, hu_ref[:, cols], 1, 1)
     logit_grad = score * (1.0 - score) * score_grad
     route_grad_ref[...] = jnp.sum(ffn_rows * logit_grad, axis=0, keepdims=True)
     rows_grad = rows_grad + logit_grad * route_ref[...]
-    down_high, down_low = split_low(down)
-    back_high, back_low = split_low(rows_grad)
+    down_ref[:routed, :], down_ref[routed:, :] = split_low(down)
+    back_ref[:routed, :], back_ref[routed:, :] = split_low(rows_grad)
+
+
+def ffn_light_kernel(
+    middle_ref,
+    input_ref,
+    cot_ref,
+    pick_ref,
+    down_ref,
+    rows_back_ref,
+    wg_ref,
+    wu_ref,
+    wd_ref,
+    back_ref,
+    block_own_ref,
+    block_send_ref,
+    *rest,
+):
+    lane_refs = rest[:-3]
+    light_grad_ref, act_ref, mix_ref = rest[-3:]
+    side = lax.axis_index("tensor")
+    half = block_own_ref.shape[0]
+    tile = 256
     width = wg_ref.shape[1]
     for first in range(0, 2):
         place = side if first == 0 else 1 - side
@@ -289,8 +339,8 @@
             act_ref[rows, :] = (gelu * up).astype(bf16)
             mix_ref[rows, :width] = (act_grad * up * slope).astype(bf16)
             mix_ref[rows, width:] = (act_grad * gelu).astype(bf16)
-            pick = pick_ref[rows, :]
-            branch = mm(act_ref[rows, :], wd_ref[...]) + (mm(pick, down_high) + mm(pick, down_low))
+            pick = jnp.concatenate([pick_ref[rows, :]] * 2, axis=1)
+            branch = mm(act_ref[rows, :], wd_ref[...]) + mm(pick, down_ref[...])
             if first == 0:
                 block_own_ref[piece, :] = middle_ref[rows, :] + branch
             else:
@@ -298,38 +348,42 @@
             back_ref[rows, :] = (
                 mm(mix_ref[rows, :width], wg_ref[...], 1, 1)
                 + mm(mix_ref[rows, width:], wu_ref[...], 1, 1)
-                + (mm(pick, back_high) + mm(pick, back_low))
+                + mm(pick, rows_back_ref[...])
             ).astype(bf16)
     light_grad_ref[:, : 2 * width] = mm(input_ref[...], mix_ref[...], 0, 0).astype(bf16)
     light_grad_ref[:, 2 * width :] = mm(cot_ref[...], act_ref[...], 0, 0).astype(bf16)
+    for lane in range(len(lane_refs) // 2):
+        lane_split(lane, lane_refs, 0, light_grad_ref, lane * width, (lane + 1) * width)
+
+
+def lane_split(lane, lane_refs, left, grad_ref, first, last):
+    bit = LANES[lane][0]
+    mine = my_bit(bit)
+    block = grad_ref.shape[0] // PARTS
+    keep_ref, send_ref = lane_refs[lane], lane_refs[len(LANES) + lane]
+    for p in range(PARTS // 2):
+        rows = slice(p * block, (p + 1) * block)
+        cols = slice(left, left + last - first)
+        for ref, value in ((keep_ref, mine), (send_ref, 1 - mine)):
+            ref[rows, cols] = grad_ref[block_rows(insert(p, bit, value), block), first:last]
 
 
 def attn_backward_kernel(
-    own_ref,
-    other_ref,
     cot_own_ref,
     cot_other_ref,
     middle_ref,
     mine_ref,
     got_ref,
-    gain_attn_ref,
     gain_ffn_ref,
     route_query_ref,
     route_key_ref,
     query_index_ref,
     key_index_ref,
-    wq_ref,
-    wk_ref,
-    wv_ref,
     wo_ref,
     hq_ref,
     hk_ref,
     hv_ref,
     ho_ref,
-    input_ref,
-    q_ref,
-    k_ref,
-    v_ref,
     result_ref,
     query_rows_ref,
     key_raw_ref,
@@ -340,26 +394,20 @@
     raw_ref,
     heavy_result_ref,
     own_middle_ref,
-    own_back_ref,
-    send_ref,
-    light_grad_ref,
-    out_grad_ref,
-    heavy_grad_ref,
+    out_ref,
+    grad_ref,
+    back_high_ref,
+    back_low_ref,
+    pick_ref,
     small_ref,
     low_ref,
-    out_ref,
-    kt_ref,
-    qt_grad_ref,
-    k_grad_ref,
-    v_grad_ref,
-    grads_ref,
-    pick_ref,
 ):
     side = lax.axis_index("tensor")
-    half = own_ref.shape[0]
+    half = cot_own_ref.shape[0]
     length = 2 * half
     tile = 256
     scale = HEAD_DIM**-0.5
+    heavy = qh_ref.shape[1]
     gain_ffn_grad = 0.0
     for cot, place, owned in ((cot_own_ref, side, True), (cot_other_ref, 1 - side, False)):
         for start in range(0, half, tile):
@@ -379,7 +427,7 @@
     for start in range(0, length, tile):
         rows = slice(start, start + tile)
         out_ref[rows, :] = mm(low_ref[rows, :], wo_ref[...], 1, 1).astype(bf16)
-    out_grad_ref[...] = mm(low_ref[...], result_ref[...], 0, 0).astype(bf16)
+    grad_ref[:, 4 * heavy :] = mm(low_ref[...], result_ref[...], 0, 0).astype(bf16)
 
     routed = query_index_ref.shape[1]
     pick_ref[:, :routed] = picks(query_index_ref, length)
@@ -389,8 +437,7 @@
     query_score = sigmoid(jnp.sum(query_rows * route_query_ref[...], axis=-1, keepdims=True))
     key_score = sigmoid(jnp.sum(key_raw * route_key_ref[...], axis=-1, keepdims=True))
     mid_rows = mm(pick_ref[:, :routed], low_ref[...], 0, 0).astype(bf16)
-    heavy = qh_ref.shape[1]
-    heavy_grad_ref[:, 3 * heavy :] = mm(mid_rows, heavy_result_ref[...], 0, 0).astype(bf16)
+    grad_ref[:, 3 * heavy : 4 * heavy] = mm(mid_rows, heavy_result_ref[...], 0, 0).astype(bf16)
     heavy_out_grad = mm(mid_rows, ho_ref[...], 1, 1).astype(bf16)
     query_score_grad = jnp.sum(
         heavy_out_grad.astype(f32) * raw_ref[...], axis=-1, keepdims=True
@@ -418,9 +465,9 @@
     query_heavy_grad = jnp.concatenate(q_parts, axis=1).astype(bf16)
     key_heavy_grad = jnp.concatenate(k_parts, axis=1).astype(bf16)
     value_heavy_grad = jnp.concatenate(v_parts, axis=1).astype(bf16)
-    heavy_grad_ref[:, :heavy] = mm(query_rows_ref[...], query_heavy_grad, 0, 0).astype(bf16)
-    heavy_grad_ref[:, heavy : 2 * heavy] = mm(key_rows_ref[...], key_heavy_grad, 0, 0).astype(bf16)
-    heavy_grad_ref[:, 2 * heavy : 3 * heavy] = mm(
+    grad_ref[:, :heavy] = mm(query_rows_ref[...], query_heavy_grad, 0, 0).astype(bf16)
+    grad_ref[:, heavy : 2 * heavy] = mm(key_rows_ref[...], key_heavy_grad, 0, 0).astype(bf16)
+    grad_ref[:, 2 * heavy : 3 * heavy] = mm(
         key_rows_ref[...], value_heavy_grad, 0, 0
     ).astype(bf16)
     key_rows_grad = mm(key_heavy_grad, hk_ref[...], 1, 1) + mm(
@@ -437,8 +484,44 @@
     small_ref[1:2, :] = 0.5 * gain_ffn_grad
     small_ref[2:3, :] = jnp.sum(query_rows * query_logit_grad, axis=0, keepdims=True)
     small_ref[3:4, :] = jnp.sum(key_raw * key_logit_grad, axis=0, keepdims=True)
-    back_high, back_low = split_low(jnp.concatenate([query_rows_grad, key_raw_grad], axis=0))
-
+    high, low = split_low(jnp.concatenate([query_rows_grad, key_raw_grad], axis=0))
+    back_high_ref[...] = high
+    back_low_ref[...] = low
+
+
+def heavy_split(cols, lane):
+    tiles = cols // 128
+    cuts = [0, (tiles + 2) // 3, 2 * ((tiles + 2) // 3), tiles]
+    return cuts[lane] * 128, cuts[lane + 1] * 128
+
+
+def light_backward_kernel(
+    own_ref,
+    other_ref,
+    wq_ref,
+    wk_ref,
+    wv_ref,
+    input_ref,
+    q_ref,
+    k_ref,
+    v_ref,
+    out_ref,
+    heavy_grad_ref,
+    back_high_ref,
+    back_low_ref,
+    pick_ref,
+    own_back_ref,
+    send_ref,
+    small_ref,
+    *rest,
+):
+    grad_refs = rest[:-6]
+    light_grad_ref, kt_ref, qt_grad_ref, k_grad_ref, v_grad_ref, mixed_ref = rest[-6:]
+    side = lax.axis_index("tensor")
+    half = own_ref.shape[0]
+    length = 2 * half
+    tile = 256
+    scale = HEAD_DIM**-0.5
     kt_ref[...] = k_ref[...].T
     k_grad_ref[...] = jnp.zeros_like(k_grad_ref)
     v_grad_ref[...] = jnp.zeros_like(v_grad_ref)
@@ -472,10 +555,11 @@
 
     lax.fori_loop(0, length // WINDOW, one_block, 0)
     light = q_ref.shape[1]
-    grads_ref[:, :light] = qt_grad_ref[...].T.astype(bf16)
-    grads_ref[:, light : 2 * light] = k_grad_ref[...].astype(bf16)
-    grads_ref[:, 2 * light :] = v_grad_ref[...].astype(bf16)
-    light_grad_ref[...] = mm(input_ref[...], grads_ref[...], 0, 0).astype(bf16)
+    mixed_ref[:, :light] = qt_grad_ref[...].T.astype(bf16)
+    mixed_ref[:, light : 2 * light] = k_grad_ref[...].astype(bf16)
+    mixed_ref[:, 2 * light :] = v_grad_ref[...].astype(bf16)
+    heavy_cols = heavy_grad_ref.shape[1]
+    light_grad = mm(input_ref[...], mixed_ref[...], 0, 0).astype(bf16)
     gain_attn_grad = 0.0
     for ref, place, owned in ((own_ref, side, True), (other_ref, 1 - side, False)):
         for start in range(0, half, tile):
@@ -483,10 +567,10 @@
             piece = slice(start, start + tile)
             pick = pick_ref[rows, :]
             back = (
-                mm(grads_ref[rows, :light], wq_ref[...], 1, 1)
-                + mm(grads_ref[rows, light : 2 * light], wk_ref[...], 1, 1)
-                + mm(grads_ref[rows, 2 * light :], wv_ref[...], 1, 1)
-                + (mm(pick, back_high) + mm(pick, back_low))
+                mm(mixed_ref[rows, :light], wq_ref[...], 1, 1)
+                + mm(mixed_ref[rows, light : 2 * light], wk_ref[...], 1, 1)
+                + mm(mixed_ref[rows, 2 * light :], wv_ref[...], 1, 1)
+                + (mm(pick, back_high_ref[...]) + mm(pick, back_low_ref[...]))
             )
             values = ref[piece, :].astype(f32)
             gain_attn_grad = gain_attn_grad + jnp.sum(
@@ -496,10 +580,102 @@
                 own_back_ref[piece, :] = back
             else:
                 send_ref[piece, :] = back.astype(bf16)
-    small_ref[0:1, :] = gain_attn_grad
-
-
-def whole(kernel, name, outs, scratch, *operands):
+    small_ref[...] = gain_attn_grad
+    if len(grad_refs) == 1:
+        grad_refs[0][:, :heavy_cols] = heavy_grad_ref[...]
+        grad_refs[0][:, heavy_cols:] = light_grad
+        return
+    light_grad_ref[...] = light_grad
+    for lane in range(len(LANES)):
+        left, right = heavy_split(heavy_cols, lane)
+        lane_split(lane, grad_refs, 0, heavy_grad_ref, left, right)
+        lane_split(lane, grad_refs, right - left, light_grad_ref, lane * light, (lane + 1) * light)
+
+
+def join_kernel(lane, send_ref, got_ref, light_ref, next_keep_ref, next_send_ref, full_ref):
+    model, heavy = full_ref.shape
+    tall = next_send_ref.shape[0]
+    light = light_ref.shape[1]
+    for wrap in range(light_ref.shape[0] // tall):
+        cols = slice(heavy + wrap * light, heavy + (wrap + 1) * light)
+        next_send_ref[:, cols] = light_ref[wrap * tall : (wrap + 1) * tall, :]
+    left = jnp.concatenate([send_ref[:, :model], got_ref[:, :model]], axis=0)
+    right = jnp.concatenate([send_ref[:, model:], got_ref[:, model:]], axis=0)
+    full_ref[...] = mm(left, right, 0, 0).astype(bf16)
+    first, second = LANES[lane][:2]
+    position = second - (1 if first < second else 0)
+    mine, next_mine = my_bit(first), my_bit(second)
+    block = model // PARTS
+    for q in range(PARTS // 4):
+        rows = slice(q * block, (q + 1) * block)
+        for ref, value in ((next_keep_ref, next_mine), (next_send_ref, 1 - next_mine)):
+            p = insert(q, position, value)
+            ref[rows, :heavy] = full_ref[block_rows(insert(p, first, mine), block), :]
+
+
+def fold_kernel(bit, position, block, *refs):
+    next_keep_ref, next_send_ref, sum_ref = refs[-3:]
+    left = 0
+    for keep_ref, got_ref in zip(refs[:-3:2], refs[1:-3:2]):
+        rows, width = keep_ref.shape
+        tall = min(rows, got_ref.shape[0])
+        skip = got_ref.shape[1] - width * (rows // tall) if tall < rows else 0
+        for wrap in range(rows // tall):
+            piece = slice(wrap * tall, (wrap + 1) * tall)
+            got = got_ref[:, skip + wrap * width : skip + (wrap + 1) * width]
+            both = keep_ref[piece, :].astype(f32) + got.astype(f32)
+            sum_ref[piece, left : left + width] = both.astype(bf16)
+        left += width
+    mine = my_bit(bit)
+    for q in range(next_keep_ref.shape[0] // block):
+        rows = slice(q * block, (q + 1) * block)
+        next_keep_ref[rows, :] = sum_ref[block_rows(insert(q, position, mine), block), :]
+        next_send_ref[rows, :] = sum_ref[block_rows(insert(q, position, 1 - mine), block), :]
+
+
+def last_fold_kernel(bit, *refs):
+    lanes = (len(refs) - 3) // 2
+    keep_ref, send_ref, sum_ref = refs[-3:]
+    left = 0
+    for lane in range(lanes):
+        width = refs[lane].shape[1]
+        both = refs[lane][...].astype(f32) + refs[lanes + lane][...].astype(f32)
+        sum_ref[:, left : left + width] = both
+        left += width
+    mine = my_bit(bit)
+    block = keep_ref.shape[0]
+    keep_ref[...] = sum_ref[block_rows(mine, block), :]
+    send_ref[...] = sum_ref[block_rows(1 - mine, block), :].astype(bf16)
+
+
+def fold(bit, position, block, *pairs):
+    rows = pairs[0].shape[0]
+    width = sum(pair.shape[1] for pair in pairs[::2])
+    return whole(
+        functools.partial(fold_kernel, bit, position, block),
+        "fold",
+        2,
+        [((rows // 2, width), bf16)] * 2,
+        [((rows, width), bf16)],
+        *pairs,
+    )
+
+
+def last_fold(bit, keeps, gots):
+    rows = keeps[0].shape[0]
+    width = sum(keep.shape[1] for keep in keeps)
+    return whole(
+        functools.partial(last_fold_kernel, bit),
+        "last_fold",
+        2,
+        [((rows // 2, width), f32), ((rows // 2, width), bf16)],
+        [((rows, width), f32)],
+        *keeps,
+        *gots,
+    )
+
+
+def whole(kernel, name, micros, outs, scratch, *operands):
     return pl.pallas_call(
         kernel,
         name=name,
@@ -508,6 +684,9 @@
         out_specs=[pl.BlockSpec(memory_space=pltpu.VMEM)] * len(outs),
         scratch_shapes=[pltpu.VMEM(shape, dtype) for shape, dtype in scratch],
         compiler_params=pltpu.CompilerParams(vmem_limit_bytes=VMEM_LIMIT),
+        cost_estimate=pl.CostEstimate(
+            flops=micros * 10**9, transcendentals=0, bytes_accessed=micros * 10**6
+        ),
     )(*operands)
 
 
@@ -562,6 +741,7 @@
     attn_partial, *saved = whole(
         attn_forward_kernel,
         "attn_forward",
+        16,
         [((length, width), bf16)] * 2
         + [((length, light), bf16)] * 4
         + [((routed, width), bf16)] * 3
@@ -577,39 +757,22 @@
         key_index,
         *attn_weights,
     )
-    (
-        middle,
-        block_own,
-        block_send,
-        ffn_back,
-        light_ffn_grad,
-        ffn_rows,
-        cot_rows,
-        act_heavy,
-        mix_heavy,
-        route_ffn_grad,
-    ) = whole(
-        ffn_kernel,
-        "ffn",
-        [
+    tuned = lax.axis_size("dp") == PARTS
+    *sends, middle, ffn_input, cot_rows, ffn_pick, down, rows_back, route_ffn_grad = whole(
+        ffn_heavy_kernel,
+        "ffn_heavy",
+        12,
+        [((routed, width + heavy_ff), bf16)] * 3
+        + [
             ((length, width), f32),
-            ((half, width), f32),
-            ((half, width), bf16),
             ((length, width), bf16),
-            ((width, 3 * light_ff), bf16),
-            ((routed, width), bf16),
-            ((routed, width), bf16),
-            ((routed, heavy_ff), bf16),
-            ((routed, 2 * heavy_ff), bf16),
+            ((length, width), bf16),
+            ((length, routed), bf16),
+            ((2 * routed, width), bf16),
+            ((2 * routed, width), bf16),
             ((1, width), f32),
         ],
-        [
-            ((length, width), bf16),
-            ((length, width), bf16),
-            ((length, light_ff), bf16),
-            ((length, 2 * light_ff), bf16),
-            ((length, routed), bf16),
-        ],
+        [],
         tokens,
         other_tokens,
         attn_partial,
@@ -619,52 +782,145 @@
         gain_ffn,
         route_ffn,
         ffn_index,
+        heavy_gate,
+        heavy_up,
+        heavy_down,
+    )
+    if tuned:
+        gots = [swap_bit(send, order[0]) for send, order in zip(sends, LANES)]
+    ffn_back, block_own, block_send, *light_parts = whole(
+        ffn_light_kernel,
+        "ffn_light",
+        12,
+        [((length, width), bf16), ((half, width), f32), ((half, width), bf16)]
+        + ([((width // 2, light_ff), bf16)] * 6 if tuned else [((width, 3 * light_ff), bf16)]),
+        ([((width, 3 * light_ff), bf16)] if tuned else [])
+        + [((length, light_ff), bf16), ((length, 2 * light_ff), bf16)],
+        middle,
+        ffn_input,
+        cot_rows,
+        ffn_pick,
+        down,
+        rows_back,
         light_gate,
         light_up,
         light_down,
-        heavy_gate,
-        heavy_up,
-        heavy_down,
-    )
-    block_out = (block_own + pair_swap(block_send).astype(f32)).astype(bf16)
-    own_middle, own_back, back_send, light_grad, out_grad, heavy_grad, small = whole(
+    )
+    back_got = pair_swap(ffn_back)
+    if tuned:
+        light_keeps = light_parts[:3]
+        light_sends = light_parts[3:]
+        token = ffn_back
+        ffn_keeps, ffn_sends = [], []
+        for lane in range(3):
+            keep, send = whole(
+                functools.partial(join_kernel, lane),
+                "join",
+                3,
+                [((width // 4, heavy_ff), bf16), ((width // 4, heavy_ff + 2 * light_ff), bf16)],
+                [((width, heavy_ff), bf16)],
+                after(token, sends[lane]),
+                gots[lane],
+                light_sends[RIDES[lane]],
+            )
+            token = keep
+            ffn_keeps.append(keep)
+            ffn_sends.append(send)
+        ffn_gots = [swap_bit(send, order[1]) for send, order in zip(ffn_sends, LANES)]
+        ffn_back = after(token, ffn_back)
+    attn_input, q_light, k_light, v_light, *routed_saved = saved
+    own_middle, out_back, heavy_grad, back_high, back_low, pick, small = whole(
         attn_backward_kernel,
         "attn_backward",
+        10,
         [
             ((half, width), f32),
-            ((half, width), f32),
-            ((half, width), bf16),
-            ((width, 3 * light), bf16),
-            ((width, light), bf16),
-            ((width, 4 * heavy), bf16),
+            ((length, light), bf16),
+            ((width, 4 * heavy + light), bf16),
+            ((2 * routed, width), bf16),
+            ((2 * routed, width), bf16),
+            ((length, 2 * routed), bf16),
             ((8, width), f32),
         ],
+        [((length, width), bf16)],
+        cotangent,
+        other_cotangent,
+        middle,
+        ffn_back,
+        back_got,
+        gain_ffn,
+        route_query,
+        route_key,
+        query_index,
+        key_index,
+        *attn_weights[3:],
+        *routed_saved,
+    )
+    block = width // lax.axis_size("dp")
+    own_back, back_send, gain_attn_grad, *attn_grads = whole(
+        light_backward_kernel,
+        "light_backward",
+        16,
+        [((half, width), f32), ((half, width), bf16), ((1, width), f32)]
+        + (
+            [
+                ((width // 2, right - left + light), bf16)
+                for left, right in [heavy_split(4 * heavy + light, lane) for lane in range(3)]
+            ]
+            * 2
+            if tuned
+            else [((width, 4 * heavy + 4 * light), bf16)]
+        ),
         [
-            ((length, width), bf16),
-            ((length, light), bf16),
+            ((width, 3 * light), bf16),
             ((light, length), bf16),
             ((light, length), f32),
             ((length, light), f32),
             ((length, light), f32),
             ((length, 3 * light), bf16),
-            ((length, 2 * routed), bf16),
         ],
         tokens,
         other_tokens,
-        cotangent,
-        other_cotangent,
-        middle,
-        ffn_back,
-        pair_swap(ffn_back),
-        gain_attn,
-        gain_ffn,
-        route_query,
-        route_key,
-        query_index,
-        key_index,
-        *attn_weights,
-        *saved,
-    )
+        *attn_weights[:3],
+        attn_input,
+        q_light,
+        k_light,
+        v_light,
+        out_back,
+        heavy_grad,
+        back_high,
+        back_low,
+        pick,
+    )
+    if tuned:
+        attn_keeps = attn_grads[:3]
+        attn_gots = [swap_bit(send, order[0]) for send, order in zip(attn_grads[3:], LANES)]
+        token = gain_attn_grad
+
+        def middle_stage(stage, token, keeps, *rest):
+            next_keeps, next_gots = [], []
+            for lane, order in enumerate(LANES):
+                left = sorted(order[stage:])
+                keep, send = fold(
+                    order[stage],
+                    left.index(order[stage]),
+                    block,
+                    after(token, keeps[lane]),
+                    *(item[lane] for item in rest),
+                )
+                token = keep
+                next_keeps.append(keep)
+                next_gots.append(swap_bit(send, order[stage]))
+            return token, next_keeps, next_gots
+
+        token, ffn_keeps, ffn_gots_next = middle_stage(2, token, ffn_keeps, ffn_gots)
+        token, attn_keeps, attn_gots = middle_stage(
+            1, token, attn_keeps, attn_gots, light_keeps, [ffn_gots[RIDES.index(i)] for i in range(3)]
+        )
+        ffn_keep, ffn_send = last_fold(3, [after(token, ffn_keeps[0]), *ffn_keeps[1:]], ffn_gots_next)
+        ffn_got = swap_bit(ffn_send, 3)
+        small = after(ffn_keep, small)
+    block_out = (block_own + pair_swap(block_send).astype(f32)).astype(bf16)
     normed_grad = own_back + pair_swap(back_send).astype(f32)
     own_tokens = tokens.astype(f32)
     factor = row_factor(own_tokens)
@@ -672,18 +928,35 @@
     gained = gain_attn * normed_grad
     inner = jnp.mean(scaled * gained, axis=-1, keepdims=True)
     input_grad = (own_middle + factor * (gained - scaled * inner)).astype(bf16)
-    small_summed = butterfly_sum(small + jnp.pad(route_ffn_grad, ((4, 3), (0, 0))))
-
-    forward_order = list(range(lax.axis_size("dp").bit_length() - 1))
-    other_order = [1, 0] + forward_order[2:]
-    heavy_mix_grad = mm(ffn_rows, mix_heavy, 0, 0).astype(bf16)
-    heavy_down_grad = mm(cot_rows, act_heavy, 0, 0).astype(bf16)
-    mixed_sum = halving_sum(heavy_mix_grad, forward_order)
-    down_sum = halving_sum(heavy_down_grad, other_order)
-    light_ffn_sum = halving_sum(light_ffn_grad, other_order)
-    heavy_sum = halving_sum(heavy_grad, forward_order)
-    light_sum = halving_sum(light_grad, other_order)
-    out_sum = halving_sum(out_grad, other_order)
+    small = small + jnp.pad(route_ffn_grad, ((4, 3), (0, 0)))
+    small_summed = butterfly_sum(small + jnp.pad(gain_attn_grad, ((0, 7), (0, 0))))
+
+    if tuned:
+        token, attn_keeps, attn_gots = middle_stage(2, small_summed, attn_keeps, attn_gots)
+        attn_keep, attn_send = last_fold(3, [after(token, attn_keeps[0]), *attn_keeps[1:]], attn_gots)
+        attn_got = swap_bit(attn_send, 3)
+        ffn_sum = ffn_keep + ffn_got.astype(f32)
+        attn_sum = attn_keep + attn_got.astype(f32)
+        hg, hu, hd = jnp.split(ffn_sum, 3, axis=1)
+        heavies, lights, ffn_lights, left = [], [], [], 0
+        for lane in range(3):
+            first, last = heavy_split(4 * heavy + light, lane)
+            for pieces, size in ((heavies, last - first), (lights, light), (ffn_lights, light_ff)):
+                pieces.append(attn_sum[:, left : left + size])
+                left += size
+        heavies = jnp.concatenate(heavies, axis=1)
+        lq, lk, lv = lights
+        lg, lu, ld = ffn_lights
+    else:
+        order = list(range(lax.axis_size("dp").bit_length() - 1))
+        hg, hu, hd = (
+            halving_sum(mm(send[:, :width], send[:, width:], 0, 0).astype(bf16), order)
+            for send in sends
+        )
+        lg, lu, ld = jnp.split(halving_sum(light_parts[0], order), 3, axis=1)
+        attn_sum = halving_sum(attn_grads[0], order)
+        heavies = attn_sum[:, : 4 * heavy + light]
+        lq, lk, lv = jnp.split(attn_sum[:, 4 * heavy + light :], 3, axis=1)
     return (
         block_out,
         input_grad,
@@ -692,20 +965,20 @@
         small_summed[2],
         small_summed[3],
         small_summed[4],
-        light_sum[:, :light],
-        light_sum[:, light : 2 * light],
-        light_sum[:, 2 * light :],
-        out_sum.T,
-        heavy_sum[:, :heavy],
-        heavy_sum[:, heavy : 2 * heavy],
-        heavy_sum[:, 2 * heavy : 3 * heavy],
-        heavy_sum[:, 3 * heavy :].T,
-        light_ffn_sum[:, :light_ff],
-        light_ffn_sum[:, light_ff : 2 * light_ff],
-        light_ffn_sum[:, 2 * light_ff :].T,
-        mixed_sum[:, :heavy_ff],
-        mixed_sum[:, heavy_ff:],
-        down_sum.T,
+        lq,
+        lk,
+        lv,
+        heavies[:, 4 * heavy :].T,
+        heavies[:, :heavy],
+        heavies[:, heavy : 2 * heavy],
+        heavies[:, 2 * heavy : 3 * heavy],
+        heavies[:, 3 * heavy : 4 * heavy].T,
+        lg,
+        lu,
+        ld.T,
+        hg,
+        hu,
+        hd.T,
     )
 
 

time: 310 us -> 242 us (0.78)
  waiting for transfers between devices: 150 us -> 62.5 us
  Pallas kernels: 65.7 us -> 118 us
  starting transfers between devices: 50.1 us -> 32.6 us
  other arithmetic: 15.7 us -> 4.16 us
    ppermute x24 -> x20, waiting for transfers between devices: 118 us -> 37.6 us  [swap_bit(): return lax.ppermute(values, 'dp', [(i, i ^ 1 << bit) for i in range(parts)])]
    pallas_call x3 -> x19, Pallas kernels: 65.7 us -> 118 us  [whole(): pl.pallas_call(kernel, name=name, out_shape=[jax.ShapeDtypeStruct(shape,...]
    ppermute x24 -> x20, starting transfers between devices: 40.9 us -> 25.7 us  [swap_bit(): return lax.ppermute(values, 'dp', [(i, i ^ 1 << bit) for i in range(parts)])]
    unnamed x40 -> x66, local copies, waits for them, and re-layouts: 2.38 us -> 11.9 us
    convert_element_type x18 -> x0, other arithmetic: 9.36 us -> none  [halving_sum(): held = held.astype(jnp.bfloat16)]
    dynamic_slice x12 -> x0, local copies, waits for them, and re-layouts: 8.76 us -> none  [the longest x6 5.37 us: halving_sum(): keep = lax.dynamic_index_in_dim(held, mine, axis, keepdims=False)]
    ppermute x4, waiting for transfers between devices: 29.2 us -> 21 us  [butterfly_sum(): lax.ppermute(values, 'dp', [(i, i ^ 1 << bit) for i in range(parts)])]
  transfers between devices with their start and end apart: 35 -> 31, of which waited for: 19 -> 10; matrix products, arithmetic and copies ran while one was open for 12% -> 4% of each run, Pallas kernels for 8% -> 30%
where the time goes in v1:
time: 242 us; the launch traced here: 238 us
  Pallas kernels  118 us (49%)
  waiting for transfers between devices  62.5 us (26%)
  starting transfers between devices  32.6 us (13%)
  local copies, waits for them, and re-layouts  19.9 us (8%)
  other arithmetic  4.16 us (2%)
    pallas_call x19, Pallas kernels, whole(): pl.pallas_call(kernel, name=name, out_shape=[jax.ShapeDtypeStruct(shape,...  118 us
    ppermute x20, waiting for transfers between devices, swap_bit(): return lax.ppermute(values, 'dp', [(i, i ^ 1 << bit) for i in range(parts)])  37.6 us
    ppermute x20, starting transfers between devices, swap_bit(): return lax.ppermute(values, 'dp', [(i, i ^ 1 << bit) for i in range(parts)])  25.7 us
    ppermute x4, waiting for transfers between devices, butterfly_sum(): lax.ppermute(values, 'dp', [(i, i ^ 1 << bit) for i in range(parts)])  21 us
    unnamed x66, local copies, waits for them, and re-layouts  11.9 us
    reshape x5, local copies, waits for them, and re-layouts, body(): item.reshape(1, -1)  4.96 us
    ppermute x4, starting transfers between devices, butterfly_sum(): lax.ppermute(values, 'dp', [(i, i ^ 1 << bit) for i in range(parts)])  4.86 us
  transfers between devices with their start and end apart: 31, of which 10 were waited for; matrix products, arithmetic and copies ran while one was open for 4% of the time, Pallas kernels for 30%

profile of v1, /device:TPU:0, one launch (start us, length us, event | category | flops | bytes accessed | tf_op | source)
XLA Modules:
  0.0 237.9 jit_solution(7140758845636496371)
XLA Ops:
  5.9 16.2 %attn_forward.1 = (bf16[1024,768]{1,0:T(8,128)(2,1)}, bf16[1024,768]{1,0:T(8,128)(2,1)}, bf16[1024,256]{1,0:T(8,128)(2,1)}, bf16[1024,256]{1,0:T(8,128)(2,1)}, b...) custom-call(bf16[512,768]{1,0:T(8,128)(2,1)} %own_ref.5, ...), custom_call_target="tpu_custom_call" | custom-call | flops 16000000000 | bytes 16000000 | tf_op jit(solution)/shard_map/attn_forward/pallas_call | solution.py:679
  28.5 12.9 %ffn_heavy.1 = (bf16[128,2816]{1,0:T(8,128)(2,1)}, bf16[128,2816]{1,0:T(8,128)(2,1)}, bf16[128,2816]{1,0:T(8,128)(2,1)}, f32[1024,768]{1,0:T(8,128)}, bf16[1024,...) custom-call(bf16[512,768]{1,0:T(8,128)(2,1)} %own_ref.5, ...), custom_call_target="tpu_custom_call" | custom-call | flops 12000000000 | bytes 12000000 | tf_op jit(solution)/shard_map/ffn_heavy/pallas_call | solution.py:679
  41.4 14.6 %ffn_light.1 = (bf16[1024,768]{1,0:T(8,128)(2,1)}, f32[512,768]{1,0:T(8,128)}, bf16[512,768]{1,0:T(8,128)(2,1)}, bf16[384,512]{1,0:T(8,128)(2,1)}, bf16[384,512]...) custom-call(f32[1024,768]{1,0:T(8,128)} %get-tuple-element.115.middl, ...), custom_call_target="tpu_custom_call" | custom-call | flops 12000000000 | bytes 12000000 | tf_op jit(solution)/shard_map/ffn_light/pallas_call | solution.py:679
  56.4 2.7 %collective-permute-start.4 = (bf16[128,2816]{1,0:T(8,128)(2,1)S(1)}, bf16[128,2816]{1,0:T(8,128)(2,1)S(1)}, u32[]{:S(2)}, u32[]{:S(2)}) collective-permute-start(bf16[128,2816]{1,0:T(8,128)(2,1)S(1)} %copy-done.21), channel_id=1, source_target_pairs={{0,2},{2,0},{4,6},{6,4},{8,10},{10,8},{12,14},{14,12},{16,18},{18,... | collective-permute-start | bytes 2162696 | tf_op jit(solution)/shard_map/ppermute | solution.py:69
  62.2 13.4 %collective-permute-done.4.got_ref = bf16[128,2816]{1,0:T(8,128)(2,1)S(1)} collective-permute-done((bf16[128,2816]{1,0:T(8,128)(2,1)S(1)}, bf16[128,2816]{1,0:T(8,128)(2,1)S(1)}, u32[]{:S(2)}, u32[]{:S(2)}) %collective-permute-start.4) | collective-permute-done | bytes 720928 | tf_op jit(solution)/shard_map/ppermute | solution.py:69
  76.5 3.8 %join.3 = (bf16[192,2048]{1,0:T(8,128)(2,1)}, bf16[192,3072]{1,0:T(8,128)(2,1)}) custom-call(bf16[128,2816]{1,0:T(8,128)(2,1)} %get-tuple-element.127.send_ref, bf16[128,2816]{1,0:T(8,128)(2,1)} %copy-done.22, bf16[384,512]{1,0:T(8,128)(2,1)} %get-tuple-element.128.light_ref), custom_call_target="tpu_custom_call" | custom-call | flops 3000000000 | bytes 3000000 | tf_op jit(solution)/shard_map/join/pallas_call | solution.py:679
  80.4 3.8 %join.4 = (bf16[192,2048]{1,0:T(8,128)(2,1)}, bf16[192,3072]{1,0:T(8,128)(2,1)}) custom-call(bf16[128,2816]{1,0:T(8,128)(2,1)} %get-tuple-element.130.send_ref, bf16[128,2816]{1,0:T(8,128)(2,1)} %collective-permute-done.5.got_ref, bf16[384,512]{1,0:T(8,128)(2,1)} %get-tuple-element.131.light_ref), custom_call_target="tpu_custom_call" | custom-call | flops 3000000000 | bytes 3000000 | tf_op jit(solution)/shard_map/join/pallas_call | solution.py:679
  84.1 3.8 %join.5 = (bf16[192,2048]{1,0:T(8,128)(2,1)}, bf16[192,3072]{1,0:T(8,128)(2,1)}) custom-call(bf16[128,2816]{1,0:T(8,128)(2,1)} %get-tuple-element.133.send_ref, bf16[128,2816]{1,0:T(8,128)(2,1)} %collective-permute-done.6.got_ref, bf16[384,512]{1,0:T(8,128)(2,1)} %get-tuple-element.134.light_ref), custom_call_target="tpu_custom_call" | custom-call | flops 3000000000 | bytes 3000000 | tf_op jit(solution)/shard_map/join/pallas_call | solution.py:679
  93.9 11.6 %attn_backward.1 = (f32[512,768]{1,0:T(8,128)}, bf16[1024,256]{1,0:T(8,128)(2,1)}, bf16[768,1792]{1,0:T(8,128)(2,1)}, bf16[256,768]{1,0:T(8,128)(2,1)}, bf16[256...) custom-call(bf16[512,768]{1,0:T(8,128)(2,1)} %cot_own_ref.3, bf16[512,768]{1,0:T(8,128)(2,1)} %copy-done.18, ...), custom_call_target="tpu_custom_call" | custom-call | flops 10000000000 | bytes 10000000 | tf_op jit(solution)/shard_map/attn_backward/pallas_call | solution.py:679
  105.5 19.5 %light_backward.1 = (f32[512,768]{1,0:T(8,128)}, bf16[512,768]{1,0:T(8,128)(2,1)}, f32[1,768]{1,0:T(1,128)}, bf16[384,896]{1,0:T(8,128)(2,1)}, bf16[384,896]{1,0...) custom-call(bf16[512,768]{1,0:T(8,128)(2,1)} %own_ref.5, ...), custom_call_target="tpu_custom_call" | custom-call | flops 16000000000 | bytes 16000000 | tf_op jit(solution)/shard_map/light_backward/pallas_call | solution.py:679
  127.5 2.9 %fold.9 = (bf16[96,2048]{1,0:T(8,128)(2,1)}, bf16[96,2048]{1,0:T(8,128)(2,1)}) custom-call(bf16[192,2048]{1,0:T(8,128)(2,1)} %get-tuple-element.160.refs_0_, bf16[192,3072]{1,0:T(8,128)(2,1)} %copy-done.15), custom_call_target="tpu_custom_call" | custom-call | flops 2000000000 | bytes 2000000 | tf_op jit(solution)/shard_map/fold/pallas_call | solution.py:679
  131.3 2.9 %fold.10 = (bf16[96,2048]{1,0:T(8,128)(2,1)}, bf16[96,2048]{1,0:T(8,128)(2,1)}) custom-call(bf16[192,2048]{1,0:T(8,128)(2,1)} %get-tuple-element.166.refs_0_, bf16[192,3072]{1,0:T(8,128)(2,1)} %copy-done.14), custom_call_target="tpu_custom_call" | custom-call | flops 2000000000 | bytes 2000000 | tf_op jit(solution)/shard_map/fold/pallas_call | solution.py:679
  134.2 2.9 %fold.11 = (bf16[96,2048]{1,0:T(8,128)(2,1)}, bf16[96,2048]{1,0:T(8,128)(2,1)}) custom-call(bf16[192,2048]{1,0:T(8,128)(2,1)} %get-tuple-element.169.refs_0_, bf16[192,3072]{1,0:T(8,128)(2,1)} %collective-permute-done.11.refs_1_.refs_3_), custom_call_target="tpu_custom_call" | custom-call | flops 2000000000 | bytes 2000000 | tf_op jit(solution)/shard_map/fold/pallas_call | solution.py:679
  139.6 4.2 %collective-permute-done.12.refs_1_ = bf16[384,896]{1,0:T(8,128)(2,1)} collective-permute-done((bf16[384,896]{1,0:T(8,128)(2,1)}, bf16[384,896]{1,0:T(8,128)(2,1)}, u32[]{:S(2)}, u32[]{:S(2)}) %collective-permute-start.12) | collective-permute-done | bytes 688160 | tf_op jit(solution)/shard_map/ppermute | solution.py:69
  143.7 3.4 %fold.12 = (bf16[192,1408]{1,0:T(8,128)(2,1)}, bf16[192,1408]{1,0:T(8,128)(2,1)}) custom-call(bf16[384,896]{1,0:T(8,128)(2,1)} %get-tuple-element.172.refs_0_, bf16[384,896]{1,0:T(8,128)(2,1)} %collective-permute-done.12.refs_1_, bf16[384,512]{1,0:T(8,128)(2,1)} %get-tuple-element.174.refs_2_, bf16[192,3072]{1,0:T(8,128)(2,1)} %collective-permute-done.11.refs_1_.refs_3_), custom_call_target="tpu_custom_call" | custom-call | flops 2000000000 | bytes 2000000 | tf_op jit(solution)/shard_map/fold/pallas_call | solution.py:679
  147.9 3.3 %fold.13 = (bf16[192,1408]{1,0:T(8,128)(2,1)}, bf16[192,1408]{1,0:T(8,128)(2,1)}) custom-call(bf16[384,896]{1,0:T(8,128)(2,1)} %get-tuple-element.176.refs_0_, bf16[384,896]{1,0:T(8,128)(2,1)} %copy-done.23, bf16[384,512]{1,0:T(8,128)(2,1)} %get-tuple-element.178.refs_2_, bf16[192,3072]{1,0:T(8,128)(2,1)} %copy-done.15), custom_call_target="tpu_custom_call" | custom-call | flops 2000000000 | bytes 2000000 | tf_op jit(solution)/shard_map/fold/pallas_call | solution.py:679
  151.3 3.2 %fold.14 = (bf16[192,1280]{1,0:T(8,128)(2,1)}, bf16[192,1280]{1,0:T(8,128)(2,1)}) custom-call(bf16[384,768]{1,0:T(8,128)(2,1)} %get-tuple-element.180.refs_0_, bf16[384,768]{1,0:T(8,128)(2,1)} %collective-permute-done.14.refs_1_, bf16[384,512]{1,0:T(8,128)(2,1)} %get-tuple-element.182.refs_2_, bf16[192,3072]{1,0:T(8,128)(2,1)} %copy-done.14), custom_call_target="tpu_custom_call" | custom-call | flops 2000000000 | bytes 2000000 | tf_op jit(solution)/shard_map/fold/pallas_call | solution.py:679
  154.6 3.4 %last_fold.2 = (f32[48,6144]{1,0:T(8,128)}, bf16[48,6144]{1,0:T(8,128)(2,1)}) custom-call(bf16[96,2048]{1,0:T(8,128)(2,1)} %get-tuple-element.184.refs_0_, bf16[96,2048]{1,0:T(8,128)(2,1)} %get-tuple-element.168.refs_1_, bf16[96,2048]{1,0:T(8,128)(2,1)} %get-tuple-element.171.refs_2_, bf16[96,2048]{1,0:T(8,128)(2,1)} %collective-permute-done.15.refs_3_, ...), custom_call_target="tpu_custom_call" | custom-call | flops 2000000000 | bytes 2000000 | tf_op jit(solution)/shard_map/last_fold/pallas_call | solution.py:679
  168.6 7.4 %collective-permute-done.20 = f32[8,768]{1,0:T(8,128)S(1)} collective-permute-done((f32[8,768]{1,0:T(8,128)S(1)}, f32[8,768]{1,0:T(8,128)S(1)}, u32[]{:S(2)}, u32[]{:S(2)}) %collective-permute-start.20) | collective-permute-done | bytes 24608 | tf_op jit(solution)/shard_map/ppermute | solution.py:45
  176.0 13.0 %collective-permute-done.21 = f32[8,768]{1,0:T(8,128)S(1)} collective-permute-done((f32[8,768]{1,0:T(8,128)S(1)}, f32[8,768]{1,0:T(8,128)S(1)}, u32[]{:S(2)}, u32[]{:S(2)}) %collective-permute-start.21) | collective-permute-done | bytes 24608 | tf_op jit(solution)/shard_map/ppermute | solution.py:45
  189.0 3.9 %collective-permute-start.22 = (f32[8,768]{1,0:T(8,128)S(1)}, f32[8,768]{1,0:T(8,128)S(1)}, u32[]{:S(2)}, u32[]{:S(2)}) collective-permute-start(f32[8,768]{1,0:T(8,128)S(1)} %add.61), channel_id=1, source_target_pairs={{0,16},{2,18},{4,20},{6,22},{8,24},{10,26},{12,28},{14,30},{16,0},... | collective-permute-start | bytes 73736 | tf_op jit(solution)/shard_map/ppermute | solution.py:45
  207.4 6.0 %collective-permute-done.28.refs_5_ = bf16[96,1280]{1,0:T(8,128)(2,1)S(1)} collective-permute-done((bf16[96,1280]{1,0:T(8,128)(2,1)}, bf16[96,1280]{1,0:T(8,128)(2,1)S(1)}, u32[]{:S(2)}, u32[]{:S(2)}) %collective-permute-start.28) | collective-permute-done | bytes 245792 | tf_op jit(solution)/shard_map/ppermute | solution.py:69
  215.5 2.8 %last_fold.3 = (f32[48,4096]{1,0:T(8,128)}, bf16[48,4096]{1,0:T(8,128)(2,1)}) custom-call(bf16[96,1408]{1,0:T(8,128)(2,1)} %get-tuple-element.200.refs_0_, bf16[96,1408]{1,0:T(8,128)(2,1)} %get-tuple-element.196.refs_1_, bf16[96,1280]{1,0:T(8,128)(2,1)} %get-tuple-element.199.refs_2_, bf16[96,1408]{1,0:T(8,128)(2,1)} %copy-done.30, ...), custom_call_target="tpu_custom_call" | custom-call | flops 2000000000 | bytes 2000000 | tf_op jit(solution)/shard_map/last_fold/pallas_call | solution.py:679
  221.6 13.9 %collective-permute-done.29 = bf16[48,4096]{1,0:T(8,128)(2,1)S(1)} collective-permute-done((bf16[48,4096]{1,0:T(8,128)(2,1)}, bf16[48,4096]{1,0:T(8,128)(2,1)S(1)}, u32[]{:S(2)}, u32[]{:S(2)}) %collective-permute-start.29) | collective-permute-done | bytes 393248 | tf_op jit(solution)/shard_map/ppermute | solution.py:69
  (148 shorter events, 61.4 us)
Async XLA Ops:
  56.1 36.7 %collective-permute-start.7 = (bf16[1024,768]{1,0:T(8,128)(2,1)}, bf16[1024,768]{1,0:T(8,128)(2,1)S(1)}, u32[]{:S(2)}, u32[]{:S(2)}) collective-permute-start(bf16[1024,768]{1,0:T(8,128)(2,1)} %get-tuple-element.136.mine_ref), channel_id=1, source_target_pairs={{0,1},{1,0},{2,3},{3,2},{4,5},{5,4},{6,7},{7,6},{8,9},{9,8},{10,11... | collective-permute-start | bytes 4718600 | tf_op jit(solution)/shard_map/ppermute | solution.py:19
  56.4 19.2 %collective-permute-start.4 = (bf16[128,2816]{1,0:T(8,128)(2,1)S(1)}, bf16[128,2816]{1,0:T(8,128)(2,1)S(1)}, u32[]{:S(2)}, u32[]{:S(2)}) collective-permute-start(bf16[128,2816]{1,0:T(8,128)(2,1)S(1)} %copy-done.21), channel_id=1, source_target_pairs={{0,2},{2,0},{4,6},{6,4},{8,10},{10,8},{12,14},{14,12},{16,18},{18,... | collective-permute-start | bytes 2162696 | tf_op jit(solution)/shard_map/ppermute | solution.py:69
  59.1 21.3 %collective-permute-start.5 = (bf16[128,2816]{1,0:T(8,128)(2,1)S(1)}, bf16[128,2816]{1,0:T(8,128)(2,1)}, u32[]{:S(2)}, u32[]{:S(2)}) collective-permute-start(bf16[128,2816]{1,0:T(8,128)(2,1)S(1)} %copy-done.20), channel_id=1, source_target_pairs={{0,4},{2,6},{4,0},{6,2},{8,12},{10,14},{12,8},{14,10},{16,20},{18,... | collective-permute-start | bytes 2162696 | tf_op jit(solution)/shard_map/ppermute | solution.py:69
  60.6 23.5 %collective-permute-start.6 = (bf16[128,2816]{1,0:T(8,128)(2,1)S(1)}, bf16[128,2816]{1,0:T(8,128)(2,1)}, u32[]{:S(2)}, u32[]{:S(2)}) collective-permute-start(bf16[128,2816]{1,0:T(8,128)(2,1)S(1)} %copy-done.19), channel_id=1, source_target_pairs={{0,8},{2,10},{4,12},{6,14},{8,0},{10,2},{12,4},{14,6},{16,24},{18,... | collective-permute-start | bytes 2162696 | tf_op jit(solution)/shard_map/ppermute | solution.py:69
  87.9 38.5 %collective-permute-start.9 = (bf16[192,3072]{1,0:T(8,128)(2,1)}, bf16[192,3072]{1,0:T(8,128)(2,1)S(1)}, u32[]{:S(2)}, u32[]{:S(2)}) collective-permute-start(bf16[192,3072]{1,0:T(8,128)(2,1)} %get-tuple-element.161), channel_id=1, source_target_pairs={{0,4},{2,6},{4,0},{6,2},{8,12},{10,14},{12,8},{14,10},{16,20},{18,... | collective-permute-start | bytes 3538952 | tf_op jit(solution)/shard_map/ppermute | solution.py:69
  89.7 40.6 %collective-permute-start.10 = (bf16[192,3072]{1,0:T(8,128)(2,1)}, bf16[192,3072]{1,0:T(8,128)(2,1)S(1)}, u32[]{:S(2)}, u32[]{:S(2)}) collective-permute-start(bf16[192,3072]{1,0:T(8,128)(2,1)} %get-tuple-element.167), channel_id=1, source_target_pairs={{0,8},{2,10},{4,12},{6,14},{8,0},{10,2},{12,4},{14,6},{16,24},{18,... | collective-permute-start | bytes 3538952 | tf_op jit(solution)/shard_map/ppermute | solution.py:69
  91.3 42.9 %collective-permute-start.11 = (bf16[192,3072]{1,0:T(8,128)(2,1)}, bf16[192,3072]{1,0:T(8,128)(2,1)}, u32[]{:S(2)}, u32[]{:S(2)}) collective-permute-start(bf16[192,3072]{1,0:T(8,128)(2,1)} %get-tuple-element.170), channel_id=1, source_target_pairs={{0,2},{2,0},{4,6},{6,4},{8,10},{10,8},{12,14},{14,12},{16,18},{18,... | collective-permute-start | bytes 3538952 | tf_op jit(solution)/shard_map/ppermute | solution.py:69
  125.0 18.7 %collective-permute-start.12 = (bf16[384,896]{1,0:T(8,128)(2,1)}, bf16[384,896]{1,0:T(8,128)(2,1)}, u32[]{:S(2)}, u32[]{:S(2)}) collective-permute-start(bf16[384,896]{1,0:T(8,128)(2,1)} %get-tuple-element.173), channel_id=1, source_target_pairs={{0,2},{2,0},{4,6},{6,4},{8,10},{10,8},{12,14},{14,12},{16,18},{18,... | collective-permute-start | bytes 2064392 | tf_op jit(solution)/shard_map/ppermute | solution.py:69
  125.8 21.3 %collective-permute-start.13 = (bf16[384,896]{1,0:T(8,128)(2,1)}, bf16[384,896]{1,0:T(8,128)(2,1)S(1)}, u32[]{:S(2)}, u32[]{:S(2)}) collective-permute-start(bf16[384,896]{1,0:T(8,128)(2,1)} %get-tuple-element.177), channel_id=1, source_target_pairs={{0,4},{2,6},{4,0},{6,2},{8,12},{10,14},{12,8},{14,10},{16,20},{18,... | collective-permute-start | bytes 2064392 | tf_op jit(solution)/shard_map/ppermute | solution.py:69
  126.4 24.9 %collective-permute-start.14 = (bf16[384,768]{1,0:T(8,128)(2,1)}, bf16[384,768]{1,0:T(8,128)(2,1)}, u32[]{:S(2)}, u32[]{:S(2)}) collective-permute-start(bf16[384,768]{1,0:T(8,128)(2,1)} %get-tuple-element.181), channel_id=1, source_target_pairs={{0,8},{2,10},{4,12},{6,14},{8,0},{10,2},{12,4},{14,6},{16,24},{18,... | collective-permute-start | bytes 1769480 | tf_op jit(solution)/shard_map/ppermute | solution.py:69
  137.1 17.5 %collective-permute-start.15 = (bf16[96,2048]{1,0:T(8,128)(2,1)}, bf16[96,2048]{1,0:T(8,128)(2,1)}, u32[]{:S(2)}, u32[]{:S(2)}) collective-permute-start(bf16[96,2048]{1,0:T(8,128)(2,1)} %get-tuple-element.185), channel_id=1, source_target_pairs={{0,8},{2,10},{4,12},{6,14},{8,0},{10,2},{12,4},{14,6},{16,24},{18,... | collective-permute-start | bytes 1179656 | tf_op jit(solution)/shard_map/ppermute | solution.py:69
  138.1 16.5 %collective-permute-start.16 = (bf16[96,2048]{1,0:T(8,128)(2,1)}, bf16[96,2048]{1,0:T(8,128)(2,1)}, u32[]{:S(2)}, u32[]{:S(2)}) collective-permute-start(bf16[96,2048]{1,0:T(8,128)(2,1)} %get-tuple-element.186), channel_id=1, source_target_pairs={{0,2},{2,0},{4,6},{6,4},{8,10},{10,8},{12,14},{14,12},{16,18},{18,... | collective-permute-start | bytes 1179656 | tf_op jit(solution)/shard_map/ppermute | solution.py:69
  143.7 10.8 %collective-permute-start.17 = (bf16[96,2048]{1,0:T(8,128)(2,1)}, bf16[96,2048]{1,0:T(8,128)(2,1)}, u32[]{:S(2)}, u32[]{:S(2)}) collective-permute-start(bf16[96,2048]{1,0:T(8,128)(2,1)} %get-tuple-element.187), channel_id=1, source_target_pairs={{0,4},{2,6},{4,0},{6,2},{8,12},{10,14},{12,8},{14,10},{16,20},{18,... | collective-permute-start | bytes 1179656 | tf_op jit(solution)/shard_map/ppermute | solution.py:69
  147.1 12.5 %collective-permute-start.3 = (bf16[512,768]{1,0:T(8,128)(2,1)}, bf16[512,768]{1,0:T(8,128)(2,1)S(1)}, u32[]{:S(2)}, u32[]{:S(2)}) collective-permute-start(bf16[512,768]{1,0:T(8,128)(2,1)} %get-tuple-element.122), channel_id=1, source_target_pairs={{0,1},{1,0},{2,3},{3,2},{4,5},{5,4},{6,7},{7,6},{8,9},{9,8},{10,11... | collective-permute-start | bytes 2359304 | tf_op jit(solution)/shard_map/ppermute | solution.py:19
  151.3 16.0 %collective-permute-start.8 = (bf16[512,768]{1,0:T(8,128)(2,1)}, bf16[512,768]{1,0:T(8,128)(2,1)S(1)}, u32[]{:S(2)}, u32[]{:S(2)}) collective-permute-start(bf16[512,768]{1,0:T(8,128)(2,1)} %get-tuple-element.157), channel_id=1, source_target_pairs={{0,1},{1,0},{2,3},{3,2},{4,5},{5,4},{6,7},{7,6},{8,9},{9,8},{10,11... | collective-permute-start | bytes 2359304 | tf_op jit(solution)/shard_map/ppermute | solution.py:19
  160.7 35.0 %collective-permute-start.23 = (bf16[192,1408]{1,0:T(8,128)(2,1)S(1)}, bf16[192,1408]{1,0:T(8,128)(2,1)S(1)}, u32[]{:S(2)}, u32[]{:S(2)}) collective-permute-start(bf16[192,1408]{1,0:T(8,128)(2,1)S(1)} %copy-done.24), channel_id=1, source_target_pairs={{0,4},{2,6},{4,0},{6,2},{8,12},{10,14},{12,8},{14,10},{16,20},{18,... | collective-permute-start | bytes 1622024 | tf_op jit(solution)/shard_map/ppermute | solution.py:69
  162.7 36.1 %collective-permute-start.24 = (bf16[192,1408]{1,0:T(8,128)(2,1)}, bf16[192,1408]{1,0:T(8,128)(2,1)S(1)}, u32[]{:S(2)}, u32[]{:S(2)}) collective-permute-start(bf16[192,1408]{1,0:T(8,128)(2,1)} %get-tuple-element.195), channel_id=1, source_target_pairs={{0,8},{2,10},{4,12},{6,14},{8,0},{10,2},{12,4},{14,6},{16,24},{18,... | collective-permute-start | bytes 1622024 | tf_op jit(solution)/shard_map/ppermute | solution.py:69
  162.7 39.2 %collective-permute-start.25 = (bf16[192,1280]{1,0:T(8,128)(2,1)}, bf16[192,1280]{1,0:T(8,128)(2,1)S(1)}, u32[]{:S(2)}, u32[]{:S(2)}) collective-permute-start(bf16[192,1280]{1,0:T(8,128)(2,1)} %get-tuple-element.198), channel_id=1, source_target_pairs={{0,2},{2,0},{4,6},{6,4},{8,10},{10,8},{12,14},{14,12},{16,18},{18,... | collective-permute-start | bytes 1474568 | tf_op jit(solution)/shard_map/ppermute | solution.py:69
  164.7 42.6 %collective-permute-start.30 = (bf16[48,6144]{1,0:T(8,128)(2,1)}, bf16[48,6144]{1,0:T(8,128)(2,1)S(1)}, u32[]{:S(2)}, u32[]{:S(2)}) collective-permute-start(bf16[48,6144]{1,0:T(8,128)(2,1)} %get-tuple-element.206), channel_id=1, source_target_pairs={{0,16},{2,18},{4,20},{6,22},{8,24},{10,26},{12,28},{14,30},{16,0},... | collective-permute-start | bytes 1769480 | tf_op jit(solution)/shard_map/ppermute | solution.py:69
  167.3 8.7 %collective-permute-start.20 = (f32[8,768]{1,0:T(8,128)S(1)}, f32[8,768]{1,0:T(8,128)S(1)}, u32[]{:S(2)}, u32[]{:S(2)}) collective-permute-start(f32[8,768]{1,0:T(8,128)S(1)} %add.59), channel_id=1, source_target_pairs={{0,4},{2,6},{4,0},{6,2},{8,12},{10,14},{12,8},{14,10},{16,20},{18,... | collective-permute-start | bytes 73736 | tf_op jit(solution)/shard_map/ppermute | solution.py:45
  176.0 13.0 %collective-permute-start.21 = (f32[8,768]{1,0:T(8,128)S(1)}, f32[8,768]{1,0:T(8,128)S(1)}, u32[]{:S(2)}, u32[]{:S(2)}) collective-permute-start(f32[8,768]{1,0:T(8,128)S(1)} %add.60), channel_id=1, source_target_pairs={{0,8},{2,10},{4,12},{6,14},{8,0},{10,2},{12,4},{14,6},{16,24},{18,... | collective-permute-start | bytes 73736 | tf_op jit(solution)/shard_map/ppermute | solution.py:45
  204.9 8.5 %collective-permute-start.26 = (bf16[96,1408]{1,0:T(8,128)(2,1)S(1)}, bf16[96,1408]{1,0:T(8,128)(2,1)S(1)}, u32[]{:S(2)}, u32[]{:S(2)}) collective-permute-start(bf16[96,1408]{1,0:T(8,128)(2,1)S(1)} %copy-done.28), channel_id=1, source_target_pairs={{0,8},{2,10},{4,12},{6,14},{8,0},{10,2},{12,4},{14,6},{16,24},{18,... | collective-permute-start | bytes 811016 | tf_op jit(solution)/shard_map/ppermute | solution.py:69
  205.4 8.7 %collective-permute-start.27 = (bf16[96,1408]{1,0:T(8,128)(2,1)S(1)}, bf16[96,1408]{1,0:T(8,128)(2,1)S(1)}, u32[]{:S(2)}, u32[]{:S(2)}) collective-permute-start(bf16[96,1408]{1,0:T(8,128)(2,1)S(1)} %copy-done.29), channel_id=1, source_target_pairs={{0,2},{2,0},{4,6},{6,4},{8,10},{10,8},{12,14},{14,12},{16,18},{18,... | collective-permute-start | bytes 811016 | tf_op jit(solution)/shard_map/ppermute | solution.py:69
  218.3 17.3 %collective-permute-start.29 = (bf16[48,4096]{1,0:T(8,128)(2,1)}, bf16[48,4096]{1,0:T(8,128)(2,1)S(1)}, u32[]{:S(2)}, u32[]{:S(2)}) collective-permute-start(bf16[48,4096]{1,0:T(8,128)(2,1)} %get-tuple-element.205), channel_id=1, source_target_pairs={{0,16},{2,18},{4,20},{6,22},{8,24},{10,26},{12,28},{14,30},{16,0},... | collective-permute-start | bytes 1179656 | tf_op jit(solution)/shard_map/ppermute | solution.py:69
  (40 other events, 257.6 us)
